TPU v7x, 32 devices: a whole 2x2x4 slice. The times are simulated.
32 devices in a mesh: mat: 8 (over z, core), pts: 4 (over y, x).
Axes of the slice: x: 2, y: 2, z: 4, core: 2. Of those that a mesh axis runs over, the one named last changes fastest.
Arguments:
- dens_blocks: bfloat16 [8, 2048, 2048], P(None, 'pts', 'mat'), may hold values from -0.00390625 to 0.00390625
- basis_values: bfloat16 [8, 6144, 1536], P('mat', 'pts'), may hold values from -6 to 6
- kernel: float32 [8, 6144], P('mat', 'pts'), may hold values from 0.3 to 3
- perturbation: float32 [8, 6144], P('mat', 'pts'), may hold values from -6 to 6
- quad_weight: float32 [8, 6144], P('mat', 'pts'), may hold values from 0.002 to 0.02
- point_count: int32 [8, 4], P('mat', 'pts'), may hold values from 192 to 1536, as said below
- active_blocks: int32 [8, 4, 12], P('mat', 'pts'), may hold values from 0 to 15, as said below
- block_pattern: int32 [8, 16, 16], replicated, may hold values 0 or 1
Outputs:
- h_response: float32 [8, 2048, 2048], P(None, 'pts', 'mat')
- n_response: float32 [8, 6144], P('mat', 'pts')
Inputs may be any that keep to these rules, and one draw needn't show every extreme that they name: `point_count`: each cluster has at least one shard with exactly 1536 points in use; the others hold 192 or more. `active_blocks`: the 12 entries of one shard are distinct block numbers of its cluster, in no particular order.
All inputs are finite; a program needn't handle non-finite values.
Results may differ from a plain program's by a relative error of at most 0.011.
Values may be sent and summed in bfloat16 or wider, within the bound.
No kernel may reach another device: no remote copies, remote signals or barrier semaphores. Data moves between devices by JAX's collectives and lax.ppermute only.
A program may use at most 128 MiB of HBM per device.

v0:
```python
import functools

import jax
import jax.numpy as jnp
from jax import lax
from jax.experimental import pallas as pl
from jax.experimental.pallas import tpu as pltpu
from jax.sharding import PartitionSpec as P


BLOCK = 128
VM = pl.BlockSpec(memory_space=pltpu.VMEM)
ANY = pl.BlockSpec(memory_space=pl.ANY)
HEAD = 3
GRANT = pltpu.CompilerParams(vmem_limit_bytes=20 << 20)


def cost(flops, moved):
    return pl.CostEstimate(flops=int(flops), bytes_accessed=int(moved), transcendentals=0)


def lanes(block):
    return pl.ds(pl.multiple_of(block * BLOCK, BLOCK), BLOCK)


def rows_at(block):
    return pl.ds(pl.multiple_of(block * BLOCK, BLOCK), BLOCK)


def pack_kernel(dims, row, meta, *refs):
    n_mat, n_pts, act, nact = dims
    arrived, packed, stage = refs[:n_mat], refs[n_mat : n_mat + n_pts], refs[-1]
    me_mat, me_pts = meta[0], meta[1]
    width = arrived[0].shape[1]
    for d in range(n_mat):
        m = lax.rem(me_mat - d + n_mat, n_mat)
        stage[:, pl.ds(pl.multiple_of(m * width, BLOCK), width)] = arrived[d][...]
    row_block = me_pts * (act // n_pts) + row
    pattern_at = HEAD + n_pts * nact + row_block * act
    for o in range(n_pts):
        for j in range(nact):
            b = meta[HEAD + o * nact + j]
            keep = meta[pattern_at + b] != 0
            value = stage[:, lanes(b)]
            packed[o][:, j * BLOCK : (j + 1) * BLOCK] = jnp.where(keep, value, jnp.zeros_like(value))


def pack(dims, row, meta, arrived, part):
    n_mat, n_pts, act, nact = dims
    width = arrived[0].shape[1]
    return pl.pallas_call(
        functools.partial(pack_kernel, dims, row),
        out_shape=[jax.ShapeDtypeStruct((BLOCK, nact * BLOCK), jnp.bfloat16)] * n_pts,
        grid_spec=pltpu.PrefetchScalarGridSpec(
            num_scalar_prefetch=1,
            grid=(1,),
            in_specs=[pl.BlockSpec((BLOCK, width), lambda i, meta: (part, 0))] * n_mat,
            out_specs=[pl.BlockSpec((BLOCK, nact * BLOCK), lambda i, meta: (0, 0))] * n_pts,
            scratch_shapes=[pltpu.VMEM((BLOCK, act * BLOCK), jnp.bfloat16)],
        ),
        compiler_params=GRANT,
        cost_estimate=cost(0, 2 * BLOCK * BLOCK * (act + n_pts * nact)),
    )(meta, *arrived)


def transpose_kernel(given, out):
    out[...] = given[...].T


def transposed(basis):
    points, orbitals = basis.shape
    tile = 256
    return pl.pallas_call(
        transpose_kernel,
        out_shape=jax.ShapeDtypeStruct((orbitals, points), basis.dtype),
        grid=(points // tile,),
        in_specs=[pl.BlockSpec((tile, orbitals), lambda i: (i, 0))],
        out_specs=pl.BlockSpec((orbitals, tile), lambda i: (0, i)),
        compiler_params=GRANT,
        cost_estimate=cost(0, 4 * points * orbitals),
        name="flip",
    )(basis)


def invert(dims, meta, place):
    _, _, act, nact = dims
    for a in range(act):
        place[a] = -1
    for i in range(nact):
        place[meta[HEAD + i]] = i


def density_kernel(dims, row, tile, meta, *refs):
    _, n_pts, act, _ = dims
    parts, flipped, before, after, place = refs[:n_pts], refs[n_pts], refs[n_pts + 1], refs[n_pts + 2], refs[n_pts + 3]
    invert(dims, meta, place)
    me_pts = meta[1]
    left = jnp.concatenate([part[...] for part in parts], axis=0)
    points = flipped.shape[1]

    @pl.loop(0, points // tile)
    def _(t):
        at = pl.ds(pl.multiple_of(t * tile, tile), tile)
        inner = jnp.dot(left, flipped[:, at], preferred_element_type=jnp.float32)
        total = before[:, at]
        for o in range(n_pts):
            spot = place[(me_pts ^ o) * (act // n_pts) + row]
            own = flipped[rows_at(jnp.maximum(spot, 0)), at].astype(jnp.float32)
            share = jnp.sum(inner[o * BLOCK : (o + 1) * BLOCK] * own, axis=0, keepdims=True)
            total = total + jnp.where(spot >= 0, share, jnp.zeros_like(share))
        after[:, at] = total


def density(dims, row, meta, parts, flipped, before):
    _, n_pts, act, _ = dims
    orbitals, points = flipped.shape
    return pl.pallas_call(
        functools.partial(density_kernel, dims, row, 256),
        out_shape=jax.ShapeDtypeStruct((1, points), jnp.float32),
        in_specs=[pl.BlockSpec(memory_space=pltpu.SMEM)] + [VM] * (n_pts + 2),
        out_specs=VM,
        scratch_shapes=[pltpu.SMEM((act,), jnp.int32)],
        compiler_params=GRANT,
        cost_estimate=cost(2 * n_pts * BLOCK * orbitals * points, 2 * orbitals * points),
    )(meta, *parts, flipped, before)


def response_kernel(dims, row, tile, meta, *refs):
    _, n_pts, act, _ = dims
    flipped, basis, raw, kern, pert, weight = refs[:6]
    out, place, left = refs[6 : 6 + n_pts], refs[-2], refs[-1]
    invert(dims, meta, place)
    me_pts = meta[1]
    points = flipped.shape[1]
    inside = lax.broadcasted_iota(jnp.int32, (1, points), 1) < meta[2]
    n = jnp.where(inside, raw[...], 0.0)
    scaling = jnp.where(inside, weight[...] * (pert[...] - kern[...] * n), 0.0)
    for o in range(n_pts):
        spot = place[(me_pts ^ o) * (act // n_pts) + row]
        own = flipped[rows_at(jnp.maximum(spot, 0)), :].astype(jnp.float32)
        scaled = jnp.where(spot >= 0, own * scaling, 0.0).astype(jnp.bfloat16)
        left[o * BLOCK : (o + 1) * BLOCK, :] = scaled

    @pl.loop(0, basis.shape[1] // tile)
    def _(t):
        at = pl.ds(pl.multiple_of(t * tile, tile), tile)
        block = jnp.dot(left[...], basis[:, at], preferred_element_type=jnp.float32)
        for o in range(n_pts):
            out[o][:, at] = block[o * BLOCK : (o + 1) * BLOCK].astype(jnp.bfloat16)


def response(dims, row, meta, flipped, basis, raw, kern, pert, weight):
    _, n_pts, act, _ = dims
    orbitals, points = flipped.shape
    return pl.pallas_call(
        functools.partial(response_kernel, dims, row, 256),
        out_shape=[jax.ShapeDtypeStruct((BLOCK, orbitals), jnp.bfloat16)] * n_pts,
        in_specs=[pl.BlockSpec(memory_space=pltpu.SMEM)] + [VM] * 6,
        out_specs=[VM] * n_pts,
        scratch_shapes=[
            pltpu.SMEM((act,), jnp.int32),
            pltpu.VMEM((n_pts * BLOCK, points), jnp.bfloat16),
        ],
        compiler_params=GRANT,
        cost_estimate=cost(2 * n_pts * BLOCK * orbitals * points, 4 * orbitals * points),
    )(meta, flipped, basis, raw, kern, pert, weight)


def combine_kernel(dims, first, count, meta, *refs):
    n_mat, n_pts, act, nact = dims
    given, out, total = refs[: count * n_pts], refs[count * n_pts : -1], refs[-1]
    me_mat, me_pts = meta[0], meta[1]
    for r in range(count):
        total[...] = jnp.zeros_like(total)
        for o in range(n_pts):
            part = given[r * n_pts + o]
            for j in range(nact):
                b = meta[HEAD + o * nact + j]
                total[:, lanes(b)] += part[:, j * BLOCK : (j + 1) * BLOCK].astype(jnp.float32)
        row_block = me_pts * (act // n_pts) + first + r
        pattern_at = HEAD + n_pts * nact + row_block * act
        for d in range(n_mat):
            m = lax.rem(me_mat + d, n_mat)
            for k in range(act // n_mat):
                b = m * (act // n_mat) + k
                keep = meta[pattern_at + b] != 0
                value = total[:, lanes(b)]
                value = jnp.where(keep, value, jnp.zeros_like(value))
                out[d][r * BLOCK : (r + 1) * BLOCK, k * BLOCK : (k + 1) * BLOCK] = value.astype(jnp.bfloat16)


def combine(dims, first, count, meta, given):
    n_mat, n_pts, act, nact = dims
    return pl.pallas_call(
        functools.partial(combine_kernel, dims, first, count),
        out_shape=[jax.ShapeDtypeStruct((count * BLOCK, act // n_mat * BLOCK), jnp.bfloat16)] * n_mat,
        in_specs=[pl.BlockSpec(memory_space=pltpu.SMEM)] + [VM] * (count * n_pts),
        out_specs=[VM] * n_mat,
        scratch_shapes=[pltpu.VMEM((BLOCK, act * BLOCK), jnp.float32)],
        compiler_params=GRANT,
        cost_estimate=cost(0, 2 * count * BLOCK * BLOCK * (act + n_pts * nact)),
    )(meta, *given)


def widen_kernel(dims, meta, *refs):
    n_mat = dims[0]
    out = refs[-1]
    for d in range(n_mat):
        c = lax.rem(meta[0] - d + n_mat, n_mat)
        out[c] = refs[d][...].astype(jnp.float32)


def widen(dims, first, count, row_blocks, meta, given, held):
    n_mat = dims[0]
    width = given[0].shape[1]
    shape = jax.ShapeDtypeStruct((n_mat, row_blocks * BLOCK, width), jnp.float32)
    whole = lambda i, meta: (0, 0)
    more = [] if held is None else [held]
    return pl.pallas_call(
        functools.partial(widen_kernel, dims),
        out_shape=shape,
        grid_spec=pltpu.PrefetchScalarGridSpec(
            num_scalar_prefetch=1,
            grid=(1,),
            in_specs=[pl.BlockSpec((count * BLOCK, width), whole)] * n_mat + [ANY] * len(more),
            out_specs=pl.BlockSpec((n_mat, count * BLOCK, width), lambda i, meta: (0, first // count, 0)),
        ),
        input_output_aliases={} if held is None else {1 + n_mat: 0},
        compiler_params=GRANT,
        cost_estimate=cost(0, 6 * count * BLOCK * n_mat * width),
    )(meta, *given, *more)


def split_rows(row_blocks, sizes):
    if sum(sizes) != row_blocks:
        sizes = [1] * row_blocks
    starts = [sum(sizes[:i]) for i in range(len(sizes))]
    return list(zip(starts, sizes))


def body(dens_blocks, basis_values, kernel, perturbation, quad_weight, point_count, active_blocks, block_pattern):
    n_mat, n_pts = lax.axis_size("mat"), lax.axis_size("pts")
    act, nact = block_pattern.shape[1], active_blocks.shape[2]
    dims = (n_mat, n_pts, act, nact)
    row_blocks = act // n_pts
    me_mat, me_pts = lax.axis_index("mat"), lax.axis_index("pts")

    def to_peer(value, o):
        return lax.ppermute(value, "pts", [(i, i ^ o) for i in range(n_pts)])

    def around(value, d):
        return lax.ppermute(value, "mat", [(i, (i + d) % n_mat) for i in range(n_mat)])

    points = basis_values.shape[1]
    basis = basis_values[0]
    own_active = active_blocks[0, 0]

    chunks_in = split_rows(row_blocks, [1, 1, 2])
    pieces = {}
    for first, count in chunks_in:
        pieces[first] = [
            lax.dynamic_slice(
                dens_blocks,
                (lax.rem(me_mat + d, n_mat), first * BLOCK, 0),
                (1, count * BLOCK, dens_blocks.shape[2]),
            )[0]
            for d in range(n_mat)
        ]
    arrived = {}

    def fetch(first):
        arrived[first] = [around(piece, d) if d else piece for d, piece in enumerate(pieces[first])]

    parts = {}

    def spread(first, part):
        row = first + part
        packed = pack(dims, row, meta, arrived[first], part)
        parts[row] = [packed[0]] + [to_peer(packed[o], o) for o in range(1, n_pts)]

    fetch(chunks_in[0][0])
    peers = [own_active] + [to_peer(own_active, o) for o in range(1, n_pts)]
    pattern = lax.dynamic_index_in_dim(block_pattern, me_mat, 0, keepdims=False).reshape(-1)
    head = jnp.stack([me_mat, me_pts, point_count[0, 0]]).astype(jnp.int32)
    meta = jnp.concatenate([head] + peers + [pattern])

    order = [(first, part) for first, count in chunks_in for part in range(count)]
    ahead = [first for first, count in chunks_in[1:]]
    for at, (first, part) in enumerate(order):
        spread(first, part)
        if at == 0:
            for later in ahead:
                fetch(later)
        if at == min(1, len(order) - 1):
            flipped = transposed(basis)

    raw = jnp.zeros((1, points), jnp.float32)
    for row in range(row_blocks):
        raw = density(dims, row, meta, parts[row], flipped, raw)

    inside = jnp.arange(points, dtype=jnp.int32)[None, :] < point_count[0, 0]
    n_response = jnp.where(inside, raw, 0.0)

    given = {}
    for row in range(row_blocks):
        sent = response(dims, row, meta, flipped, basis, raw, kernel, perturbation, quad_weight)
        given[row] = [sent[0]] + [to_peer(sent[o], o) for o in range(1, n_pts)]

    chunks_out = split_rows(row_blocks, [2, 1, 1])
    back = {}
    for first, count in chunks_out:
        cut = combine(dims, first, count, meta, sum([given[first + r] for r in range(count)], []))
        back[first] = [cut[0]] + [around(cut[d], d) for d in range(1, n_mat)]
    held = None
    for first, count in chunks_out:
        held = widen(dims, first, count, row_blocks, meta, back[first], held)
    return held, n_response


def solution(mesh):
    placed = (
        P(None, "pts", "mat"),
        P("mat", "pts", None),
        P("mat", "pts"),
        P("mat", "pts"),
        P("mat", "pts"),
        P("mat", "pts"),
        P("mat", "pts", None),
        P(),
    )

    return jax.shard_map(
        body,
        mesh=mesh,
        in_specs=placed,
        out_specs=(P(None, "pts", "mat"), P("mat", "pts")),
        check_vma=False,
    )
```

profile of v0, /device:TPU:0, one launch (start us, length us, event | category | flops | bytes accessed | tf_op | source)
XLA Modules:
  0.0 244.9 jit_solution(5675590781005424794)
XLA Ops:
  2.0 4.6 %collective-permute-start.32 = (bf16[128,256]{1,0:T(8,128)(2,1)S(1)}, bf16[128,256]{1,0:T(8,128)(2,1)S(1)}, u32[]{:S(2)}, u32[]{:S(2)}) collective-permute-start(bf16[128,256]{1,0:T(8,128)(2,1)S(1)} %get-tuple-element.114), channel_id=1, source_target_pairs={{0,28},{4,0},{8,4},{12,8},{16,12},{20,16},{24,20},{28,24},{1,29},{... | collective-permute-start | bytes 196616 | tf_op jit(solution)/shard_map/ppermute | solution.py:252
  14.3 3.1 %collective-permute-start.22 = (bf16[128,256]{1,0:T(8,128)(2,1)S(1)}, bf16[128,256]{1,0:T(8,128)(2,1)S(1)}, u32[]{:S(2)}, u32[]{:S(2)}) collective-permute-start(bf16[128,256]{1,0:T(8,128)(2,1)S(1)} %get-tuple-element.121), channel_id=1, source_target_pairs={{0,28},{4,0},{8,4},{12,8},{16,12},{20,16},{24,20},{28,24},{1,29},{... | collective-permute-start | bytes 196616 | tf_op jit(solution)/shard_map/ppermute | solution.py:252
  33.3 5.0 %collective-permute-done.31.refs_6_ = bf16[128,256]{1,0:T(8,128)(2,1)S(1)} collective-permute-done((bf16[128,256]{1,0:T(8,128)(2,1)S(1)}, bf16[128,256]{1,0:T(8,128)(2,1)S(1)}, u32[]{:S(2)}, u32[]{:S(2)}) %collective-permute-start.31) | collective-permute-done | bytes 65568 | tf_op jit(solution)/shard_map/ppermute | solution.py:252
  40.0 2.5 %collective-permute-start.33 = (bf16[128,1536]{1,0:T(8,128)(2,1)S(1)}, bf16[128,1536]{1,0:T(8,128)(2,1)S(1)}, u32[]{:S(2)}, u32[]{:S(2)}) collective-permute-start(bf16[128,1536]{1,0:T(8,128)(2,1)S(1)} %get-tuple-element.71), channel_id=1, source_target_pairs={{0,1},{1,0},{2,3},{3,2},{4,5},{5,4},{6,7},{7,6},{8,9},{9,8},{10,11... | collective-permute-start | bytes 1179656 | tf_op jit(solution)/shard_map/ppermute | solution.py:249
  45.4 3.3 %collective-permute-start.4 = (bf16[256,256]{1,0:T(8,128)(2,1)S(1)}, bf16[256,256]{1,0:T(8,128)(2,1)S(1)}, u32[]{:S(2)}, u32[]{:S(2)}) collective-permute-start(bf16[256,256]{1,0:T(8,128)(2,1)S(1)} %get-tuple-element.135), channel_id=1, source_target_pairs={{0,8},{4,12},{8,16},{12,20},{16,24},{20,28},{24,0},{28,4},{1,9},{5... | collective-permute-start | bytes 393224 | tf_op jit(solution)/shard_map/ppermute | solution.py:252
  49.7 9.5 %collective-permute-done.6.refs_4_ = bf16[256,256]{1,0:T(8,128)(2,1)S(1)} collective-permute-done((bf16[256,256]{1,0:T(8,128)(2,1)S(1)}, bf16[256,256]{1,0:T(8,128)(2,1)S(1)}, u32[]{:S(2)}, u32[]{:S(2)}) %collective-permute-start.6) | collective-permute-done | bytes 131104 | tf_op jit(solution)/shard_map/ppermute | solution.py:252
  61.3 6.2 %collective-permute-done.3.refs_1_ = bf16[256,256]{1,0:T(8,128)(2,1)S(1)} collective-permute-done((bf16[256,256]{1,0:T(8,128)(2,1)S(1)}, bf16[256,256]{1,0:T(8,128)(2,1)S(1)}, u32[]{:S(2)}, u32[]{:S(2)}) %collective-permute-start.3) | collective-permute-done | bytes 131104 | tf_op jit(solution)/shard_map/ppermute | solution.py:252
  80.9 4.2 %shard_map.99.refs_5_ = f32[1,1536]{1,0:T(1,128)S(1)} custom-call(s32[307]{0:T(512)S(1)} %concatenate.3.meta, bf16[128,1536]{1,0:T(8,128)(2,1)S(1)} %get-tuple-element.70.refs_0_, bf16[128,1536]{1,0:T(8,128)(2,1)S(1)} %collective-permute-done.33.refs_1_, bf16[128,1536]{1,0:T(8,128)(2,1)S(1)} %collective-permute-done.34.refs_2_, ...), custom_call_target="tpu_custom_call" | custom-call | flops 2415919104 | bytes 4718592 | tf_op jit(solution)/shard_map/pallas_call | solution.py:117
  85.2 2.7 %collective-permute-done.24.refs_2_ = bf16[128,1536]{1,0:T(8,128)(2,1)S(1)} collective-permute-done((bf16[128,1536]{1,0:T(8,128)(2,1)S(1)}, bf16[128,1536]{1,0:T(8,128)(2,1)S(1)}, u32[]{:S(2)}, u32[]{:S(2)}) %collective-permute-start.24) | collective-permute-done | bytes 393248 | tf_op jit(solution)/shard_map/ppermute | solution.py:249
  89.9 6.7 %collective-permute-done.13.refs_1_ = bf16[128,1536]{1,0:T(8,128)(2,1)S(1)} collective-permute-done((bf16[128,1536]{1,0:T(8,128)(2,1)S(1)}, bf16[128,1536]{1,0:T(8,128)(2,1)S(1)}, u32[]{:S(2)}, u32[]{:S(2)}) %collective-permute-start.13) | collective-permute-done | bytes 393248 | tf_op jit(solution)/shard_map/ppermute | solution.py:249
  97.8 4.2 %shard_map.100.refs_5_ = f32[1,1536]{1,0:T(1,128)S(1)} custom-call(s32[307]{0:T(512)S(1)} %concatenate.3.meta, bf16[128,1536]{1,0:T(8,128)(2,1)S(1)} %get-tuple-element.66.refs_0_, bf16[128,1536]{1,0:T(8,128)(2,1)S(1)} %collective-permute-done.23.refs_1_, bf16[128,1536]{1,0:T(8,128)(2,1)S(1)} %collective-permute-done.24.refs_2_, ...), custom_call_target="tpu_custom_call" | custom-call | flops 2415919104 | bytes 4718592 | tf_op jit(solution)/shard_map/pallas_call | solution.py:117
  102.1 2.6 %collective-permute-done.14.refs_2_ = bf16[128,1536]{1,0:T(8,128)(2,1)S(1)} collective-permute-done((bf16[128,1536]{1,0:T(8,128)(2,1)S(1)}, bf16[128,1536]{1,0:T(8,128)(2,1)S(1)}, u32[]{:S(2)}, u32[]{:S(2)}) %collective-permute-start.14) | collective-permute-done | bytes 393248 | tf_op jit(solution)/shard_map/ppermute | solution.py:249
  106.0 4.2 %shard_map.101.refs_5_ = f32[1,1536]{1,0:T(1,128)S(1)} custom-call(s32[307]{0:T(512)S(1)} %concatenate.3.meta, bf16[128,1536]{1,0:T(8,128)(2,1)S(1)} %get-tuple-element.62.refs_0_, bf16[128,1536]{1,0:T(8,128)(2,1)S(1)} %collective-permute-done.13.refs_1_, bf16[128,1536]{1,0:T(8,128)(2,1)S(1)} %collective-permute-done.14.refs_2_, ...), custom_call_target="tpu_custom_call" | custom-call | flops 2415919104 | bytes 4718592 | tf_op jit(solution)/shard_map/pallas_call | solution.py:117
  110.3 3.2 %collective-permute-done.10.refs_1_ = bf16[128,1536]{1,0:T(8,128)(2,1)S(1)} collective-permute-done((bf16[128,1536]{1,0:T(8,128)(2,1)S(1)}, bf16[128,1536]{1,0:T(8,128)(2,1)S(1)}, u32[]{:S(2)}, u32[]{:S(2)}) %collective-permute-start.10) | collective-permute-done | bytes 393248 | tf_op jit(solution)/shard_map/ppermute | solution.py:249
  114.2 7.8 %collective-permute-done.12.refs_3_ = bf16[128,1536]{1,0:T(8,128)(2,1)S(1)} collective-permute-done((bf16[128,1536]{1,0:T(8,128)(2,1)S(1)}, bf16[128,1536]{1,0:T(8,128)(2,1)S(1)}, u32[]{:S(2)}, u32[]{:S(2)}) %collective-permute-start.12) | collective-permute-done | bytes 393248 | tf_op jit(solution)/shard_map/ppermute | solution.py:249
  122.0 4.2 %shard_map.102.refs_2_ = f32[1,1536]{1,0:T(1,128)S(1)} custom-call(s32[307]{0:T(512)S(1)} %concatenate.3.meta, bf16[128,1536]{1,0:T(8,128)(2,1)S(1)} %get-tuple-element.58.refs_0_, bf16[128,1536]{1,0:T(8,128)(2,1)S(1)} %collective-permute-done.10.refs_1_, bf16[128,1536]{1,0:T(8,128)(2,1)S(1)} %collective-permute-done.11.refs_2_, ...), custom_call_target="tpu_custom_call" | custom-call | flops 2415919104 | bytes 4718592 | tf_op jit(solution)/shard_map/pallas_call | solution.py:117
  126.3 4.4 %shard_map.108 = (bf16[128,1536]{1,0:T(8,128)(2,1)S(1)}, bf16[128,1536]{1,0:T(8,128)(2,1)S(1)}, bf16[128,1536]{1,0:T(8,128)(2,1)S(1)}, bf16[128,1536]{1,0:T(8,128)(2,1)S(1)}) custom-call(s32[307]{0:T(512)S(1)} %concatenate.3.meta, bf16[1536,1536]{1,0:T(8,128)(2,1)S(1)} %flip.1.refs_4_.refs_0_, bf16[1536,1536]{1,0:T(8,128)(2,1)S(1)} %bitcast.59, ...), custom_call_target="tpu_custom_call" | custom-call | flops 2415919104 | bytes 9437184 | tf_op jit(solution)/shard_map/pallas_call | solution.py:155
  134.3 4.4 %shard_map.107 = (bf16[128,1536]{1,0:T(8,128)(2,1)S(1)}, bf16[128,1536]{1,0:T(8,128)(2,1)S(1)}, bf16[128,1536]{1,0:T(8,128)(2,1)S(1)}, bf16[128,1536]{1,0:T(8,128)(2,1)S(1)}) custom-call(s32[307]{0:T(512)S(1)} %concatenate.3.meta, bf16[1536,1536]{1,0:T(8,128)(2,1)S(1)} %flip.1.refs_4_.refs_0_, bf16[1536,1536]{1,0:T(8,128)(2,1)S(1)} %bitcast.60, ...), custom_call_target="tpu_custom_call" | custom-call | flops 2415919104 | bytes 9437184 | tf_op jit(solution)/shard_map/pallas_call | solution.py:155
  139.1 4.4 %shard_map.105 = (bf16[128,1536]{1,0:T(8,128)(2,1)S(1)}, bf16[128,1536]{1,0:T(8,128)(2,1)S(1)}, bf16[128,1536]{1,0:T(8,128)(2,1)S(1)}, bf16[128,1536]{1,0:T(8,128)(2,1)S(1)}) custom-call(s32[307]{0:T(512)S(1)} %concatenate.3.meta, bf16[1536,1536]{1,0:T(8,128)(2,1)S(1)} %flip.1.refs_4_.refs_0_, bf16[1536,1536]{1,0:T(8,128)(2,1)S(1)} %bitcast.61, ...), custom_call_target="tpu_custom_call" | custom-call | flops 2415919104 | bytes 9437184 | tf_op jit(solution)/shard_map/pallas_call | solution.py:155
  148.0 3.2 %collective-permute-start.48 = (bf16[128,1536]{1,0:T(8,128)(2,1)S(1)}, bf16[128,1536]{1,0:T(8,128)(2,1)S(1)}, u32[]{:S(2)}, u32[]{:S(2)}) collective-permute-start(bf16[128,1536]{1,0:T(8,128)(2,1)S(1)} %get-tuple-element.89), channel_id=1, source_target_pairs={{0,3},{1,2},{2,1},{3,0},{4,7},{5,6},{6,5},{7,4},{8,11},{9,10},{10,... | collective-permute-start | bytes 1179656 | tf_op jit(solution)/shard_map/ppermute | solution.py:249
  151.3 2.6 %collective-permute-start.57 = (bf16[128,1536]{1,0:T(8,128)(2,1)S(1)}, bf16[128,1536]{1,0:T(8,128)(2,1)S(1)}, u32[]{:S(2)}, u32[]{:S(2)}) collective-permute-start(bf16[128,1536]{1,0:T(8,128)(2,1)S(1)} %get-tuple-element.100), channel_id=1, source_target_pairs={{0,2},{1,3},{2,0},{3,1},{4,6},{5,7},{6,4},{7,5},{8,10},{9,11},{10,... | collective-permute-start | bytes 1179656 | tf_op jit(solution)/shard_map/ppermute | solution.py:249
  153.9 4.4 %shard_map.103 = (bf16[128,1536]{1,0:T(8,128)(2,1)S(1)}, bf16[128,1536]{1,0:T(8,128)(2,1)S(1)}, bf16[128,1536]{1,0:T(8,128)(2,1)S(1)}, bf16[128,1536]{1,0:T(8,128)(2,1)S(1)}) custom-call(s32[307]{0:T(512)S(1)} %concatenate.3.meta, bf16[1536,1536]{1,0:T(8,128)(2,1)S(1)} %flip.1.refs_4_.refs_0_, bf16[1536,1536]{1,0:T(8,128)(2,1)S(1)} %bitcast.62, ...), custom_call_target="tpu_custom_call" | custom-call | flops 2415919104 | bytes 9437184 | tf_op jit(solution)/shard_map/pallas_call | solution.py:155
  160.2 7.9 %collective-permute-done.46.refs_1_ = bf16[128,1536]{1,0:T(8,128)(2,1)S(1)} collective-permute-done((bf16[128,1536]{1,0:T(8,128)(2,1)S(1)}, bf16[128,1536]{1,0:T(8,128)(2,1)S(1)}, u32[]{:S(2)}, u32[]{:S(2)}) %collective-permute-start.46) | collective-permute-done | bytes 393248 | tf_op jit(solution)/shard_map/ppermute | solution.py:249
  169.2 7.4 %collective-permute-done.48.refs_3_ = bf16[128,1536]{1,0:T(8,128)(2,1)S(1)} collective-permute-done((bf16[128,1536]{1,0:T(8,128)(2,1)S(1)}, bf16[128,1536]{1,0:T(8,128)(2,1)S(1)}, u32[]{:S(2)}, u32[]{:S(2)}) %collective-permute-start.48) | collective-permute-done | bytes 393248 | tf_op jit(solution)/shard_map/ppermute | solution.py:249
  179.2 3.2 %collective-permute-done.57.refs_2_ = bf16[128,1536]{1,0:T(8,128)(2,1)S(1)} collective-permute-done((bf16[128,1536]{1,0:T(8,128)(2,1)S(1)}, bf16[128,1536]{1,0:T(8,128)(2,1)S(1)}, u32[]{:S(2)}, u32[]{:S(2)}) %collective-permute-start.57) | collective-permute-done | bytes 393248 | tf_op jit(solution)/shard_map/ppermute | solution.py:249
  182.5 2.5 %collective-permute-done.58.refs_3_ = bf16[128,1536]{1,0:T(8,128)(2,1)S(1)} collective-permute-done((bf16[128,1536]{1,0:T(8,128)(2,1)S(1)}, bf16[128,1536]{1,0:T(8,128)(2,1)S(1)}, u32[]{:S(2)}, u32[]{:S(2)}) %collective-permute-start.58) | collective-permute-done | bytes 393248 | tf_op jit(solution)/shard_map/ppermute | solution.py:249
  185.0 8.5 %collective-permute-done.36.refs_1_ = bf16[128,1536]{1,0:T(8,128)(2,1)S(1)} collective-permute-done((bf16[128,1536]{1,0:T(8,128)(2,1)S(1)}, bf16[128,1536]{1,0:T(8,128)(2,1)S(1)}, u32[]{:S(2)}, u32[]{:S(2)}) %collective-permute-start.36) | collective-permute-done | bytes 393248 | tf_op jit(solution)/shard_map/ppermute | solution.py:249
  193.5 6.7 %collective-permute-done.38.refs_3_ = bf16[128,1536]{1,0:T(8,128)(2,1)S(1)} collective-permute-done((bf16[128,1536]{1,0:T(8,128)(2,1)S(1)}, bf16[128,1536]{1,0:T(8,128)(2,1)S(1)}, u32[]{:S(2)}, u32[]{:S(2)}) %collective-permute-start.38) | collective-permute-done | bytes 393248 | tf_op jit(solution)/shard_map/ppermute | solution.py:249
  206.2 3.0 %collective-permute-start.55 = (bf16[128,256]{1,0:T(8,128)(2,1)S(1)}, bf16[128,256]{1,0:T(8,128)(2,1)S(1)}, u32[]{:S(2)}, u32[]{:S(2)}) collective-permute-start(bf16[128,256]{1,0:T(8,128)(2,1)S(1)} %get-tuple-element.97), channel_id=1, source_target_pairs={{0,28},{4,0},{8,4},{12,8},{16,12},{20,16},{24,20},{28,24},{1,29},{... | collective-permute-start | bytes 196616 | tf_op jit(solution)/shard_map/ppermute | solution.py:252
  219.5 5.2 %collective-permute-done.64.refs_3_ = bf16[256,256]{1,0:T(8,128)(2,1)S(1)} collective-permute-done((bf16[256,256]{1,0:T(8,128)(2,1)S(1)}, bf16[256,256]{1,0:T(8,128)(2,1)S(1)}, u32[]{:S(2)}, u32[]{:S(2)}) %collective-permute-start.64) | collective-permute-done | bytes 131104 | tf_op jit(solution)/shard_map/ppermute | solution.py:252
  225.8 6.0 %collective-permute-start.43 = (bf16[128,256]{1,0:T(8,128)(2,1)S(1)}, bf16[128,256]{1,0:T(8,128)(2,1)S(1)}, u32[]{:S(2)}, u32[]{:S(2)}) collective-permute-start(bf16[128,256]{1,0:T(8,128)(2,1)S(1)} %get-tuple-element.83), channel_id=1, source_target_pairs={{0,20},{4,24},{8,28},{12,0},{16,4},{20,8},{24,12},{28,16},{1,21},{... | collective-permute-start | bytes 196616 | tf_op jit(solution)/shard_map/ppermute | solution.py:252
  231.9 5.4 %collective-permute-start.44 = (bf16[128,256]{1,0:T(8,128)(2,1)S(1)}, bf16[128,256]{1,0:T(8,128)(2,1)S(1)}, u32[]{:S(2)}, u32[]{:S(2)}) collective-permute-start(bf16[128,256]{1,0:T(8,128)(2,1)S(1)} %get-tuple-element.84), channel_id=1, source_target_pairs={{0,24},{4,28},{8,0},{12,4},{16,8},{20,12},{24,16},{28,20},{1,25},{... | collective-permute-start | bytes 196616 | tf_op jit(solution)/shard_map/ppermute | solution.py:252
  (149 shorter events, 89.6 us)
Async XLA Ops:
  25.8 18.2 %collective-permute-start.9 = (bf16[256,256]{1,0:T(8,128)(2,1)S(1)}, bf16[256,256]{1,0:T(8,128)(2,1)S(1)}, u32[]{:S(2)}, u32[]{:S(2)}) collective-permute-start(bf16[256,256]{1,0:T(8,128)(2,1)S(1)} %get-tuple-element.130), channel_id=1, source_target_pairs={{0,28},{4,0},{8,4},{12,8},{16,12},{20,16},{24,20},{28,24},{1,29},{... | collective-permute-start | bytes 393224 | tf_op jit(solution)/shard_map/ppermute | solution.py:252
  27.9 17.0 %collective-permute-start.8 = (bf16[256,256]{1,0:T(8,128)(2,1)S(1)}, bf16[256,256]{1,0:T(8,128)(2,1)S(1)}, u32[]{:S(2)}, u32[]{:S(2)}) collective-permute-start(bf16[256,256]{1,0:T(8,128)(2,1)S(1)} %get-tuple-element.131), channel_id=1, source_target_pairs={{0,24},{4,28},{8,0},{12,4},{16,8},{20,12},{24,16},{28,20},{1,25},{... | collective-permute-start | bytes 393224 | tf_op jit(solution)/shard_map/ppermute | solution.py:252
  40.0 30.1 %collective-permute-start.33 = (bf16[128,1536]{1,0:T(8,128)(2,1)S(1)}, bf16[128,1536]{1,0:T(8,128)(2,1)S(1)}, u32[]{:S(2)}, u32[]{:S(2)}) collective-permute-start(bf16[128,1536]{1,0:T(8,128)(2,1)S(1)} %get-tuple-element.71), channel_id=1, source_target_pairs={{0,1},{1,0},{2,3},{3,2},{4,5},{5,4},{6,7},{7,6},{8,9},{9,8},{10,11... | collective-permute-start | bytes 1179656 | tf_op jit(solution)/shard_map/ppermute | solution.py:249
  42.4 29.2 %collective-permute-start.34 = (bf16[128,1536]{1,0:T(8,128)(2,1)S(1)}, bf16[128,1536]{1,0:T(8,128)(2,1)S(1)}, u32[]{:S(2)}, u32[]{:S(2)}) collective-permute-start(bf16[128,1536]{1,0:T(8,128)(2,1)S(1)} %get-tuple-element.72), channel_id=1, source_target_pairs={{0,2},{1,3},{2,0},{3,1},{4,6},{5,7},{6,4},{7,5},{8,10},{9,11},{10,... | collective-permute-start | bytes 1179656 | tf_op jit(solution)/shard_map/ppermute | solution.py:249
  44.8 16.0 %collective-permute-start.5 = (bf16[256,256]{1,0:T(8,128)(2,1)S(1)}, bf16[256,256]{1,0:T(8,128)(2,1)S(1)}, u32[]{:S(2)}, u32[]{:S(2)}) collective-permute-start(bf16[256,256]{1,0:T(8,128)(2,1)S(1)} %get-tuple-element.134), channel_id=1, source_target_pairs={{0,12},{4,16},{8,20},{12,24},{16,28},{20,0},{24,4},{28,8},{1,13},{... | collective-permute-start | bytes 393224 | tf_op jit(solution)/shard_map/ppermute | solution.py:252
  59.3 18.1 %collective-permute-start.35 = (bf16[128,1536]{1,0:T(8,128)(2,1)S(1)}, bf16[128,1536]{1,0:T(8,128)(2,1)S(1)}, u32[]{:S(2)}, u32[]{:S(2)}) collective-permute-start(bf16[128,1536]{1,0:T(8,128)(2,1)S(1)} %get-tuple-element.73), channel_id=1, source_target_pairs={{0,3},{1,2},{2,1},{3,0},{4,7},{5,6},{6,5},{7,4},{8,11},{9,10},{10,... | collective-permute-start | bytes 1179656 | tf_op jit(solution)/shard_map/ppermute | solution.py:249
  60.8 18.9 %collective-permute-start.23 = (bf16[128,1536]{1,0:T(8,128)(2,1)S(1)}, bf16[128,1536]{1,0:T(8,128)(2,1)S(1)}, u32[]{:S(2)}, u32[]{:S(2)}) collective-permute-start(bf16[128,1536]{1,0:T(8,128)(2,1)S(1)} %get-tuple-element.67), channel_id=1, source_target_pairs={{0,1},{1,0},{2,3},{3,2},{4,5},{5,4},{6,7},{7,6},{8,9},{9,8},{10,11... | collective-permute-start | bytes 1179656 | tf_op jit(solution)/shard_map/ppermute | solution.py:249
  67.5 20.4 %collective-permute-start.24 = (bf16[128,1536]{1,0:T(8,128)(2,1)S(1)}, bf16[128,1536]{1,0:T(8,128)(2,1)S(1)}, u32[]{:S(2)}, u32[]{:S(2)}) collective-permute-start(bf16[128,1536]{1,0:T(8,128)(2,1)S(1)} %get-tuple-element.68), channel_id=1, source_target_pairs={{0,2},{1,3},{2,0},{3,1},{4,6},{5,7},{6,4},{7,5},{8,10},{9,11},{10,... | collective-permute-start | bytes 1179656 | tf_op jit(solution)/shard_map/ppermute | solution.py:249
  70.0 19.4 %collective-permute-start.25 = (bf16[128,1536]{1,0:T(8,128)(2,1)S(1)}, bf16[128,1536]{1,0:T(8,128)(2,1)S(1)}, u32[]{:S(2)}, u32[]{:S(2)}) collective-permute-start(bf16[128,1536]{1,0:T(8,128)(2,1)S(1)} %get-tuple-element.69), channel_id=1, source_target_pairs={{0,3},{1,2},{2,1},{3,0},{4,7},{5,6},{6,5},{7,4},{8,11},{9,10},{10,... | collective-permute-start | bytes 1179656 | tf_op jit(solution)/shard_map/ppermute | solution.py:249
  71.6 25.0 %collective-permute-start.13 = (bf16[128,1536]{1,0:T(8,128)(2,1)S(1)}, bf16[128,1536]{1,0:T(8,128)(2,1)S(1)}, u32[]{:S(2)}, u32[]{:S(2)}) collective-permute-start(bf16[128,1536]{1,0:T(8,128)(2,1)S(1)} %get-tuple-element.63), channel_id=1, source_target_pairs={{0,1},{1,0},{2,3},{3,2},{4,5},{5,4},{6,7},{7,6},{8,9},{9,8},{10,11... | collective-permute-start | bytes 1179656 | tf_op jit(solution)/shard_map/ppermute | solution.py:249
  77.4 27.3 %collective-permute-start.14 = (bf16[128,1536]{1,0:T(8,128)(2,1)S(1)}, bf16[128,1536]{1,0:T(8,128)(2,1)S(1)}, u32[]{:S(2)}, u32[]{:S(2)}) collective-permute-start(bf16[128,1536]{1,0:T(8,128)(2,1)S(1)} %get-tuple-element.64), channel_id=1, source_target_pairs={{0,2},{1,3},{2,0},{3,1},{4,6},{5,7},{6,4},{7,5},{8,10},{9,11},{10,... | collective-permute-start | bytes 1179656 | tf_op jit(solution)/shard_map/ppermute | solution.py:249
  79.7 26.3 %collective-permute-start.15 = (bf16[128,1536]{1,0:T(8,128)(2,1)S(1)}, bf16[128,1536]{1,0:T(8,128)(2,1)S(1)}, u32[]{:S(2)}, u32[]{:S(2)}) collective-permute-start(bf16[128,1536]{1,0:T(8,128)(2,1)S(1)} %get-tuple-element.65), channel_id=1, source_target_pairs={{0,3},{1,2},{2,1},{3,0},{4,7},{5,6},{6,5},{7,4},{8,11},{9,10},{10,... | collective-permute-start | bytes 1179656 | tf_op jit(solution)/shard_map/ppermute | solution.py:249
  87.8 25.7 %collective-permute-start.10 = (bf16[128,1536]{1,0:T(8,128)(2,1)S(1)}, bf16[128,1536]{1,0:T(8,128)(2,1)S(1)}, u32[]{:S(2)}, u32[]{:S(2)}) collective-permute-start(bf16[128,1536]{1,0:T(8,128)(2,1)S(1)} %get-tuple-element.59), channel_id=1, source_target_pairs={{0,1},{1,0},{2,3},{3,2},{4,5},{5,4},{6,7},{7,6},{8,9},{9,8},{10,11... | collective-permute-start | bytes 1179656 | tf_op jit(solution)/shard_map/ppermute | solution.py:249
  89.4 24.7 %collective-permute-start.11 = (bf16[128,1536]{1,0:T(8,128)(2,1)S(1)}, bf16[128,1536]{1,0:T(8,128)(2,1)S(1)}, u32[]{:S(2)}, u32[]{:S(2)}) collective-permute-start(bf16[128,1536]{1,0:T(8,128)(2,1)S(1)} %get-tuple-element.60), channel_id=1, source_target_pairs={{0,2},{1,3},{2,0},{3,1},{4,6},{5,7},{6,4},{7,5},{8,10},{9,11},{10,... | collective-permute-start | bytes 1179656 | tf_op jit(solution)/shard_map/ppermute | solution.py:249
  96.6 25.4 %collective-permute-start.12 = (bf16[128,1536]{1,0:T(8,128)(2,1)S(1)}, bf16[128,1536]{1,0:T(8,128)(2,1)S(1)}, u32[]{:S(2)}, u32[]{:S(2)}) collective-permute-start(bf16[128,1536]{1,0:T(8,128)(2,1)S(1)} %get-tuple-element.61), channel_id=1, source_target_pairs={{0,3},{1,2},{2,1},{3,0},{4,7},{5,6},{6,5},{7,4},{8,11},{9,10},{10,... | collective-permute-start | bytes 1179656 | tf_op jit(solution)/shard_map/ppermute | solution.py:249
  131.1 16.9 %collective-permute-start.60 = (bf16[128,1536]{1,0:T(8,128)(2,1)S(1)}, bf16[128,1536]{1,0:T(8,128)(2,1)S(1)}, u32[]{:S(2)}, u32[]{:S(2)}) collective-permute-start(bf16[128,1536]{1,0:T(8,128)(2,1)S(1)} %get-tuple-element.104), channel_id=1, source_target_pairs={{0,2},{1,3},{2,0},{3,1},{4,6},{5,7},{6,4},{7,5},{8,10},{9,11},{10,... | collective-permute-start | bytes 1179656 | tf_op jit(solution)/shard_map/ppermute | solution.py:249
  131.9 19.4 %collective-permute-start.61 = (bf16[128,1536]{1,0:T(8,128)(2,1)S(1)}, bf16[128,1536]{1,0:T(8,128)(2,1)S(1)}, u32[]{:S(2)}, u32[]{:S(2)}) collective-permute-start(bf16[128,1536]{1,0:T(8,128)(2,1)S(1)} %get-tuple-element.105), channel_id=1, source_target_pairs={{0,3},{1,2},{2,1},{3,0},{4,7},{5,6},{6,5},{7,4},{8,11},{9,10},{10,... | collective-permute-start | bytes 1179656 | tf_op jit(solution)/shard_map/ppermute | solution.py:249
  138.7 21.0 %collective-permute-start.56 = (bf16[128,1536]{1,0:T(8,128)(2,1)S(1)}, bf16[128,1536]{1,0:T(8,128)(2,1)S(1)}, u32[]{:S(2)}, u32[]{:S(2)}) collective-permute-start(bf16[128,1536]{1,0:T(8,128)(2,1)S(1)} %get-tuple-element.99), channel_id=1, source_target_pairs={{0,1},{1,0},{2,3},{3,2},{4,5},{5,4},{6,7},{7,6},{8,9},{9,8},{10,11... | collective-permute-start | bytes 1179656 | tf_op jit(solution)/shard_map/ppermute | solution.py:249
  143.5 24.6 %collective-permute-start.46 = (bf16[128,1536]{1,0:T(8,128)(2,1)S(1)}, bf16[128,1536]{1,0:T(8,128)(2,1)S(1)}, u32[]{:S(2)}, u32[]{:S(2)}) collective-permute-start(bf16[128,1536]{1,0:T(8,128)(2,1)S(1)} %get-tuple-element.87), channel_id=1, source_target_pairs={{0,1},{1,0},{2,3},{3,2},{4,5},{5,4},{6,7},{7,6},{8,9},{9,8},{10,11... | collective-permute-start | bytes 1179656 | tf_op jit(solution)/shard_map/ppermute | solution.py:249
  145.3 23.1 %collective-permute-start.47 = (bf16[128,1536]{1,0:T(8,128)(2,1)S(1)}, bf16[128,1536]{1,0:T(8,128)(2,1)S(1)}, u32[]{:S(2)}, u32[]{:S(2)}) collective-permute-start(bf16[128,1536]{1,0:T(8,128)(2,1)S(1)} %get-tuple-element.88), channel_id=1, source_target_pairs={{0,2},{1,3},{2,0},{3,1},{4,6},{5,7},{6,4},{7,5},{8,10},{9,11},{10,... | collective-permute-start | bytes 1179656 | tf_op jit(solution)/shard_map/ppermute | solution.py:249
  148.0 28.6 %collective-permute-start.48 = (bf16[128,1536]{1,0:T(8,128)(2,1)S(1)}, bf16[128,1536]{1,0:T(8,128)(2,1)S(1)}, u32[]{:S(2)}, u32[]{:S(2)}) collective-permute-start(bf16[128,1536]{1,0:T(8,128)(2,1)S(1)} %get-tuple-element.89), channel_id=1, source_target_pairs={{0,3},{1,2},{2,1},{3,0},{4,7},{5,6},{6,5},{7,4},{8,11},{9,10},{10,... | collective-permute-start | bytes 1179656 | tf_op jit(solution)/shard_map/ppermute | solution.py:249
  151.3 31.2 %collective-permute-start.57 = (bf16[128,1536]{1,0:T(8,128)(2,1)S(1)}, bf16[128,1536]{1,0:T(8,128)(2,1)S(1)}, u32[]{:S(2)}, u32[]{:S(2)}) collective-permute-start(bf16[128,1536]{1,0:T(8,128)(2,1)S(1)} %get-tuple-element.100), channel_id=1, source_target_pairs={{0,2},{1,3},{2,0},{3,1},{4,6},{5,7},{6,4},{7,5},{8,10},{9,11},{10,... | collective-permute-start | bytes 1179656 | tf_op jit(solution)/shard_map/ppermute | solution.py:249
  159.7 25.3 %collective-permute-start.58 = (bf16[128,1536]{1,0:T(8,128)(2,1)S(1)}, bf16[128,1536]{1,0:T(8,128)(2,1)S(1)}, u32[]{:S(2)}, u32[]{:S(2)}) collective-permute-start(bf16[128,1536]{1,0:T(8,128)(2,1)S(1)} %get-tuple-element.101), channel_id=1, source_target_pairs={{0,3},{1,2},{2,1},{3,0},{4,7},{5,6},{6,5},{7,4},{8,11},{9,10},{10,... | collective-permute-start | bytes 1179656 | tf_op jit(solution)/shard_map/ppermute | solution.py:249
  168.1 25.3 %collective-permute-start.36 = (bf16[128,1536]{1,0:T(8,128)(2,1)S(1)}, bf16[128,1536]{1,0:T(8,128)(2,1)S(1)}, u32[]{:S(2)}, u32[]{:S(2)}) collective-permute-start(bf16[128,1536]{1,0:T(8,128)(2,1)S(1)} %get-tuple-element.75), channel_id=1, source_target_pairs={{0,1},{1,0},{2,3},{3,2},{4,5},{5,4},{6,7},{7,6},{8,9},{9,8},{10,11... | collective-permute-start | bytes 1179656 | tf_op jit(solution)/shard_map/ppermute | solution.py:249
  168.4 25.0 %collective-permute-start.37 = (bf16[128,1536]{1,0:T(8,128)(2,1)S(1)}, bf16[128,1536]{1,0:T(8,128)(2,1)S(1)}, u32[]{:S(2)}, u32[]{:S(2)}) collective-permute-start(bf16[128,1536]{1,0:T(8,128)(2,1)S(1)} %get-tuple-element.76), channel_id=1, source_target_pairs={{0,2},{1,3},{2,0},{3,1},{4,6},{5,7},{6,4},{7,5},{8,10},{9,11},{10,... | collective-permute-start | bytes 1179656 | tf_op jit(solution)/shard_map/ppermute | solution.py:249
  176.6 23.6 %collective-permute-start.38 = (bf16[128,1536]{1,0:T(8,128)(2,1)S(1)}, bf16[128,1536]{1,0:T(8,128)(2,1)S(1)}, u32[]{:S(2)}, u32[]{:S(2)}) collective-permute-start(bf16[128,1536]{1,0:T(8,128)(2,1)S(1)} %get-tuple-element.77), channel_id=1, source_target_pairs={{0,3},{1,2},{2,1},{3,0},{4,7},{5,6},{6,5},{7,4},{8,11},{9,10},{10,... | collective-permute-start | bytes 1179656 | tf_op jit(solution)/shard_map/ppermute | solution.py:249
  182.5 17.7 %collective-permute-start.49 = (bf16[128,256]{1,0:T(8,128)(2,1)S(1)}, bf16[128,256]{1,0:T(8,128)(2,1)S(1)}, u32[]{:S(2)}, u32[]{:S(2)}) collective-permute-start(bf16[128,256]{1,0:T(8,128)(2,1)S(1)} %get-tuple-element.91), channel_id=1, source_target_pairs={{0,4},{4,8},{8,12},{12,16},{16,20},{20,24},{24,28},{28,0},{1,5},{5... | collective-permute-start | bytes 196616 | tf_op jit(solution)/shard_map/ppermute | solution.py:252
  185.0 18.6 %collective-permute-start.50 = (bf16[128,256]{1,0:T(8,128)(2,1)S(1)}, bf16[128,256]{1,0:T(8,128)(2,1)S(1)}, u32[]{:S(2)}, u32[]{:S(2)}) collective-permute-start(bf16[128,256]{1,0:T(8,128)(2,1)S(1)} %get-tuple-element.92), channel_id=1, source_target_pairs={{0,8},{4,12},{8,16},{12,20},{16,24},{20,28},{24,0},{28,4},{1,9},{5... | collective-permute-start | bytes 196616 | tf_op jit(solution)/shard_map/ppermute | solution.py:252
  217.8 19.5 %collective-permute-start.68 = (bf16[256,256]{1,0:T(8,128)(2,1)S(1)}, bf16[256,256]{1,0:T(8,128)(2,1)S(1)}, u32[]{:S(2)}, u32[]{:S(2)}) collective-permute-start(bf16[256,256]{1,0:T(8,128)(2,1)S(1)} %get-tuple-element.113), channel_id=1, source_target_pairs={{0,28},{4,0},{8,4},{12,8},{16,12},{20,16},{24,20},{28,24},{1,29},{... | collective-permute-start | bytes 393224 | tf_op jit(solution)/shard_map/ppermute | solution.py:252
  224.7 18.5 %collective-permute-start.41 = (bf16[128,256]{1,0:T(8,128)(2,1)S(1)}, bf16[128,256]{1,0:T(8,128)(2,1)S(1)}, u32[]{:S(2)}, u32[]{:S(2)}) collective-permute-start(bf16[128,256]{1,0:T(8,128)(2,1)S(1)} %get-tuple-element.81), channel_id=1, source_target_pairs={{0,12},{4,16},{8,20},{12,24},{16,28},{20,0},{24,4},{28,8},{1,13},{... | collective-permute-start | bytes 196616 | tf_op jit(solution)/shard_map/ppermute | solution.py:252
  225.8 17.5 %collective-permute-start.42 = (bf16[128,256]{1,0:T(8,128)(2,1)S(1)}, bf16[128,256]{1,0:T(8,128)(2,1)S(1)}, u32[]{:S(2)}, u32[]{:S(2)}) collective-permute-start(bf16[128,256]{1,0:T(8,128)(2,1)S(1)} %get-tuple-element.82), channel_id=1, source_target_pairs={{0,16},{4,20},{8,24},{12,28},{16,0},{20,4},{24,8},{28,12},{1,17},{... | collective-permute-start | bytes 196616 | tf_op jit(solution)/shard_map/ppermute | solution.py:252
  225.8 17.5 %collective-permute-start.43 = (bf16[128,256]{1,0:T(8,128)(2,1)S(1)}, bf16[128,256]{1,0:T(8,128)(2,1)S(1)}, u32[]{:S(2)}, u32[]{:S(2)}) collective-permute-start(bf16[128,256]{1,0:T(8,128)(2,1)S(1)} %get-tuple-element.83), channel_id=1, source_target_pairs={{0,20},{4,24},{8,28},{12,0},{16,4},{20,8},{24,12},{28,16},{1,21},{... | collective-permute-start | bytes 196616 | tf_op jit(solution)/shard_map/ppermute | solution.py:252
  (45 other events, 470.8 us)
where the time goes:
time: 246 us; the launch traced here: 245 us
  waiting for transfers between devices  104 us (42%)
  starting transfers between devices  82.3 us (33%)
  Pallas kernels  50.8 us (21%)
  local copies, waits for them, and re-layouts  5.21 us (2%)
    ppermute x27, waiting for transfers between devices, to_peer(): return lax.ppermute(value, 'pts', [(i, i ^ o) for i in range(n_pts)])  68.8 us
    ppermute x42, starting transfers between devices, around(): lax.ppermute(value, 'mat', [(i, (i + d) % n_mat) for i in range(n_mat)])  49.3 us
    ppermute x42, waiting for transfers between devices, around(): lax.ppermute(value, 'mat', [(i, (i + d) % n_mat) for i in range(n_mat)])  35.5 us
    ppermute x27, starting transfers between devices, to_peer(): return lax.ppermute(value, 'pts', [(i, i ^ o) for i in range(n_pts)])  32.9 us
    pallas_call x4, Pallas kernels, response(): pl.pallas_call(functools.partial(response_kernel, dims, row, 256), out_sh...  17.7 us
    pallas_call x4, Pallas kernels, density(): pl.pallas_call(functools.partial(density_kernel, dims, row, 256), out_sha...  16.9 us
    pallas_call x3, Pallas kernels, widen(): pl.pallas_call(functools.partial(widen_kernel, dims), out_shape=shape, gr...  5.23 us
    pallas_call x3, Pallas kernels, combine(): pl.pallas_call(functools.partial(combine_kernel, dims, first, count), out...  4.92 us
  transfers between devices with their start and end apart: 69, of which 32 were waited for; matrix products, arithmetic and copies ran while one was open for 1% of the time, Pallas kernels for 17%

commit v1 on v0

v1 whole, which is shorter than its diff:
```python
import functools

import jax
import jax.numpy as jnp
from jax import lax
from jax.experimental import pallas as pl
from jax.experimental.pallas import tpu as pltpu
from jax.sharding import PartitionSpec as P


BLOCK = 128
VM = pl.BlockSpec(memory_space=pltpu.VMEM)
ANY = pl.BlockSpec(memory_space=pl.ANY)
HEAD = 3
GRANT = pltpu.CompilerParams(vmem_limit_bytes=20 << 20)


def cost(flops, moved):
    return pl.CostEstimate(flops=int(flops), bytes_accessed=int(moved), transcendentals=0)


def lanes(block):
    return pl.ds(pl.multiple_of(block * BLOCK, BLOCK), BLOCK)


def pack_kernel(dims, start, single, meta, *refs):
    n_mat, n_pts, act, nact = dims
    each = act // n_mat
    if single:
        arrived, packed = refs[0], refs[1:]
    else:
        packed, stage = refs[n_mat:-1], refs[-1]
        for d in range(n_mat):
            stage[meta[0] ^ d] = refs[d][...]
        arrived = stage
    row_block = meta[1] * (act // n_pts) + start // BLOCK
    pattern_at = HEAD + n_pts * nact + row_block * act
    for o in range(n_pts):
        for j in range(nact):
            b = meta[HEAD + o * nact + j]
            keep = meta[pattern_at + b] != 0
            value = arrived[b // each, :, lanes(lax.rem(b, each))]
            packed[o][:, j * BLOCK : (j + 1) * BLOCK] = jnp.where(keep, value, jnp.zeros_like(value))


def pack(dims, start, rows, meta, arrived, skip):
    n_mat, n_pts, act, nact = dims
    single = not isinstance(arrived, list)
    width = act // n_mat * BLOCK
    if single:
        given = [pl.BlockSpec((n_mat, rows, width), lambda i, meta: (0, skip // rows, 0))]
        scratch = []
    else:
        given = [pl.BlockSpec((rows, width), lambda i, meta: (skip // rows, 0))] * n_mat
        scratch = [pltpu.VMEM((n_mat, rows, width), jnp.bfloat16)]
    return pl.pallas_call(
        functools.partial(pack_kernel, dims, start, single),
        out_shape=[jax.ShapeDtypeStruct((rows, nact * BLOCK), jnp.bfloat16)] * n_pts,
        grid_spec=pltpu.PrefetchScalarGridSpec(
            num_scalar_prefetch=1,
            grid=(1,),
            in_specs=given,
            out_specs=[pl.BlockSpec((rows, nact * BLOCK), lambda i, meta: (0, 0))] * n_pts,
            scratch_shapes=scratch,
        ),
        compiler_params=GRANT,
        cost_estimate=cost(0, 2 * rows * BLOCK * (act + n_pts * nact)),
    )(meta, *([arrived] if single else arrived))


def transpose_kernel(given, out):
    out[...] = given[...].T


def transposed(basis):
    points, orbitals = basis.shape
    tile = 256
    return pl.pallas_call(
        transpose_kernel,
        out_shape=jax.ShapeDtypeStruct((orbitals, points), basis.dtype),
        grid=(points // tile,),
        in_specs=[pl.BlockSpec((tile, orbitals), lambda i: (i, 0))],
        out_specs=pl.BlockSpec((orbitals, tile), lambda i: (0, i)),
        compiler_params=GRANT,
        cost_estimate=cost(0, 4 * points * orbitals),
        name="flip",
    )(basis)


def invert(dims, meta, place):
    _, _, act, nact = dims
    for a in range(act):
        place[a] = -1
    for i in range(nact):
        place[meta[HEAD + i]] = i


def rows_of(place, block, start, rows):
    spot = place[block]
    at = jnp.maximum(spot, 0) * BLOCK + start % BLOCK
    return pl.ds(pl.multiple_of(at, rows), rows), spot >= 0


def density_kernel(dims, start, rows, tile, meta, *refs):
    _, n_pts, act, _ = dims
    parts, flipped, before, after, place = refs[:n_pts], refs[n_pts], refs[n_pts + 1], refs[n_pts + 2], refs[n_pts + 3]
    invert(dims, meta, place)
    left = jnp.concatenate([part[...] for part in parts], axis=0)
    points = flipped.shape[1]

    @pl.loop(0, points // tile)
    def _(t):
        at = pl.ds(pl.multiple_of(t * tile, tile), tile)
        inner = jnp.dot(left, flipped[:, at], preferred_element_type=jnp.float32)
        total = before[:, at]
        for o in range(n_pts):
            where, active = rows_of(place, (meta[1] ^ o) * (act // n_pts) + start // BLOCK, start, rows)
            own = flipped[where, at].astype(jnp.float32)
            share = jnp.sum(inner[o * rows : (o + 1) * rows] * own, axis=0, keepdims=True)
            total = total + jnp.where(active, share, jnp.zeros_like(share))
        after[:, at] = total


def density(dims, start, rows, meta, parts, flipped, before):
    _, n_pts, act, _ = dims
    orbitals, points = flipped.shape
    return pl.pallas_call(
        functools.partial(density_kernel, dims, start, rows, 256),
        out_shape=jax.ShapeDtypeStruct((1, points), jnp.float32),
        in_specs=[pl.BlockSpec(memory_space=pltpu.SMEM)] + [VM] * (n_pts + 2),
        out_specs=VM,
        scratch_shapes=[pltpu.SMEM((act,), jnp.int32)],
        compiler_params=GRANT,
        cost_estimate=cost(2 * n_pts * rows * orbitals * points, 2 * orbitals * points),
    )(meta, *parts, flipped, before)


def response_kernel(dims, start, rows, tile, meta, *refs):
    _, n_pts, act, _ = dims
    flipped, basis, raw, kern, pert, weight = refs[:6]
    out, place, left = refs[6 : 6 + n_pts], refs[-2], refs[-1]
    invert(dims, meta, place)
    points = flipped.shape[1]
    inside = lax.broadcasted_iota(jnp.int32, (1, points), 1) < meta[2]
    n = jnp.where(inside, raw[...], 0.0)
    scaling = jnp.where(inside, weight[...] * (pert[...] - kern[...] * n), 0.0)
    for o in range(n_pts):
        where, active = rows_of(place, (meta[1] ^ o) * (act // n_pts) + start // BLOCK, start, rows)
        own = flipped[where, :].astype(jnp.float32)
        left[o * rows : (o + 1) * rows, :] = jnp.where(active, own * scaling, 0.0).astype(jnp.bfloat16)

    @pl.loop(0, basis.shape[1] // tile)
    def _(t):
        at = pl.ds(pl.multiple_of(t * tile, tile), tile)
        block = jnp.dot(left[...], basis[:, at], preferred_element_type=jnp.float32)
        for o in range(n_pts):
            out[o][:, at] = block[o * rows : (o + 1) * rows].astype(jnp.bfloat16)


def response(dims, start, rows, meta, flipped, basis, raw, kern, pert, weight):
    _, n_pts, act, _ = dims
    orbitals, points = flipped.shape
    return pl.pallas_call(
        functools.partial(response_kernel, dims, start, rows, 256),
        out_shape=[jax.ShapeDtypeStruct((rows, orbitals), jnp.bfloat16)] * n_pts,
        in_specs=[pl.BlockSpec(memory_space=pltpu.SMEM)] + [VM] * 6,
        out_specs=[VM] * n_pts,
        scratch_shapes=[
            pltpu.SMEM((act,), jnp.int32),
            pltpu.VMEM((n_pts * rows, points), jnp.bfloat16),
        ],
        compiler_params=GRANT,
        cost_estimate=cost(2 * n_pts * rows * orbitals * points, 4 * orbitals * points),
    )(meta, flipped, basis, raw, kern, pert, weight)


def combine_kernel(dims, strips, single, meta, *refs):
    n_mat, n_pts, act, nact = dims
    given = len(strips) * n_pts
    out, total = refs[given:-1], refs[-1]
    each = act // n_mat
    done = 0
    for s, (start, rows) in enumerate(strips):
        total[...] = jnp.zeros_like(total)
        for o in range(n_pts):
            part = refs[s * n_pts + o]
            for j in range(nact):
                b = meta[HEAD + o * nact + j]
                total[:rows, lanes(b)] += part[:, j * BLOCK : (j + 1) * BLOCK].astype(jnp.float32)
        row_block = meta[1] * (act // n_pts) + start // BLOCK
        pattern_at = HEAD + n_pts * nact + row_block * act
        for d in range(n_mat):
            m = d if single else meta[0] ^ d
            for k in range(each):
                b = m * each + k
                keep = meta[pattern_at + b] != 0
                value = total[:rows, lanes(b)]
                value = jnp.where(keep, value, jnp.zeros_like(value)).astype(jnp.bfloat16)
                to = out[0].at[d] if single else out[d]
                to[done : done + rows, k * BLOCK : (k + 1) * BLOCK] = value
        done += rows


def combine(dims, strips, single, meta, given):
    n_mat, n_pts, act, nact = dims
    rows = sum(rows for start, rows in strips)
    width = act // n_mat * BLOCK
    if single:
        shapes = [jax.ShapeDtypeStruct((n_mat, rows, width), jnp.bfloat16)]
    else:
        shapes = [jax.ShapeDtypeStruct((rows, width), jnp.bfloat16)] * n_mat
    return pl.pallas_call(
        functools.partial(combine_kernel, dims, strips, single),
        out_shape=shapes,
        in_specs=[pl.BlockSpec(memory_space=pltpu.SMEM)] + [VM] * len(given),
        out_specs=[VM] * len(shapes),
        scratch_shapes=[pltpu.VMEM((BLOCK, act * BLOCK), jnp.float32)],
        compiler_params=GRANT,
        cost_estimate=cost(0, 2 * rows * BLOCK * (act + n_pts * nact)),
    )(meta, *given)


def widen_kernel(single, n_mat, meta, *refs):
    out = refs[-1]
    if single:
        out[...] = refs[0][...].astype(jnp.float32)
    else:
        for d in range(n_mat):
            out[meta[0] ^ d] = refs[d][...].astype(jnp.float32)


def widen(dims, start, rows, all_rows, meta, given, held):
    n_mat, _, act, _ = dims
    single = not isinstance(given, list)
    width = act // n_mat * BLOCK
    if single:
        specs, given = [pl.BlockSpec((n_mat, rows, width), lambda i, meta: (0, 0, 0))], [given]
    else:
        specs = [pl.BlockSpec((rows, width), lambda i, meta: (0, 0))] * n_mat
    more = [] if held is None else [held]
    return pl.pallas_call(
        functools.partial(widen_kernel, single, n_mat),
        out_shape=jax.ShapeDtypeStruct((n_mat, all_rows, width), jnp.float32),
        grid_spec=pltpu.PrefetchScalarGridSpec(
            num_scalar_prefetch=1,
            grid=(1,),
            in_specs=specs + [ANY] * len(more),
            out_specs=pl.BlockSpec((n_mat, rows, width), lambda i, meta: (0, start // rows, 0)),
        ),
        input_output_aliases={} if held is None else {1 + len(given): 0},
        compiler_params=GRANT,
        cost_estimate=cost(0, 6 * rows * n_mat * width),
    )(meta, *given, *more)


def chunks(row_blocks, shape):
    half = BLOCK // 2
    if sum(sum(sizes) for single, sizes in shape) != 2 * row_blocks:
        shape = [(False, [2])] * row_blocks
    out, at = [], 0
    for single, sizes in shape:
        strips = []
        for size in sizes:
            strips.append((at, size * half))
            at += size * half
        out.append((single, tuple(strips)))
    return out


def plan_of(row_blocks):
    inward = chunks(row_blocks, [(False, [2]), (False, [2]), (True, [2, 1, 1])])
    outward = chunks(row_blocks, [(True, [1, 1]), (True, [2]), (True, [2]), (False, [1]), (False, [1])])
    return inward, outward


def body(dens_blocks, basis_values, kernel, perturbation, quad_weight, point_count, active_blocks, block_pattern):
    n_mat, n_pts = lax.axis_size("mat"), lax.axis_size("pts")
    act, nact = block_pattern.shape[1], active_blocks.shape[2]
    dims = (n_mat, n_pts, act, nact)
    inward, outward = plan_of(act // n_pts)
    me_mat, me_pts = lax.axis_index("mat"), lax.axis_index("pts")

    def to_peer(value, o):
        return lax.ppermute(value, "pts", [(i, i ^ o) for i in range(n_pts)])

    points = basis_values.shape[1]
    basis = basis_values[0]
    own_active = active_blocks[0, 0]

    def across(single, values):
        if single:
            return lax.all_to_all(values, "mat", 0, 0, tiled=True)
        return [
            lax.ppermute(value, "mat", [(i, i ^ d) for i in range(n_mat)]) if d else value
            for d, value in enumerate(values)
        ]

    arrived = {}
    for single, strips in inward:
        start, rows = strips[0][0], sum(rows for at, rows in strips)
        cut = dens_blocks[:, start : start + rows]
        if not single:
            cut = [
                lax.dynamic_slice(dens_blocks, (me_mat ^ d, start, 0), (1, rows, dens_blocks.shape[2]))[0]
                for d in range(n_mat)
            ]
        arrived[start] = across(single, cut)

    peers = [own_active] + [to_peer(own_active, o) for o in range(1, n_pts)]
    pattern = lax.dynamic_index_in_dim(block_pattern, me_mat, 0, keepdims=False).reshape(-1)
    head = jnp.stack([me_mat, me_pts, point_count[0, 0]]).astype(jnp.int32)
    meta = jnp.concatenate([head] + peers + [pattern])

    flipped = transposed(basis)

    parts = {}
    for single, strips in inward:
        first = strips[0][0]
        for start, rows in strips:
            packed = pack(dims, start, rows, meta, arrived[first], start - first)
            parts[start] = [packed[0]] + [to_peer(packed[o], o) for o in range(1, n_pts)]

    raw = jnp.zeros((1, points), jnp.float32)
    for single, strips in inward:
        for start, rows in strips:
            raw = density(dims, start, rows, meta, parts[start], flipped, raw)

    inside = jnp.arange(points, dtype=jnp.int32)[None, :] < point_count[0, 0]
    n_response = jnp.where(inside, raw, 0.0)

    given = {}
    for single, strips in outward:
        for start, rows in strips:
            sent = response(dims, start, rows, meta, flipped, basis, raw, kernel, perturbation, quad_weight)
            given[start] = [sent[0]] + [to_peer(sent[o], o) for o in range(1, n_pts)]

    held = None
    for single, strips in outward:
        start, rows = strips[0][0], sum(rows for at, rows in strips)
        cut = combine(dims, strips, single, meta, sum([given[at] for at, rows in strips], []))
        back = across(single, cut[0] if single else cut)
        held = widen(dims, start, rows, dens_blocks.shape[1], meta, back, held)
    return held, n_response


def solution(mesh):
    placed = (
        P(None, "pts", "mat"),
        P("mat", "pts", None),
        P("mat", "pts"),
        P("mat", "pts"),
        P("mat", "pts"),
        P("mat", "pts"),
        P("mat", "pts", None),
        P(),
    )

    return jax.shard_map(
        body,
        mesh=mesh,
        in_specs=placed,
        out_specs=(P(None, "pts", "mat"), P("mat", "pts")),
        check_vma=False,
    )
```

time: 246 us -> 294 us (1.20)
  local copies, waits for them, and re-layouts: 5.21 us -> 25.2 us
  Pallas kernels: 50.8 us -> 65.3 us
  starting transfers between devices: 82.3 us -> 96.3 us
    all_to_all x0 -> x4, starting transfers between devices: none -> 19.5 us  [across(): return lax.all_to_all(values, 'mat', 0, 0, tiled=True)]
    unnamed x16 -> x40, local copies, waits for them, and re-layouts: 2.37 us -> 21.7 us
    ppermute x42 -> x28, starting transfers between devices: 49.3 us -> 32.9 us  [across(): lax.ppermute(value, 'mat', [(i, i ^ d) for i in range(n_mat)])]
    pallas_call x18 -> x26, Pallas kernels: 48.9 us -> 63.3 us  [the longest x6 20.9 us: response(): pl.pallas_call(functools.partial(response_kernel, dims, start, rows, 256)...]
    ppermute x27 -> x36, starting transfers between devices: 32.9 us -> 43.9 us  [to_peer(): return lax.ppermute(value, 'pts', [(i, i ^ o) for i in range(n_pts)])]
    ppermute x42 -> x28, waiting for transfers between devices: 35.5 us -> 32 us  [across(): lax.ppermute(value, 'mat', [(i, i ^ d) for i in range(n_mat)])]
    ppermute x27 -> x36, waiting for transfers between devices: 68.8 us -> 71.8 us  [to_peer(): return lax.ppermute(value, 'pts', [(i, i ^ o) for i in range(n_pts)])]
  transfers between devices with their start and end apart: 69 -> 68, of which waited for: 32 -> 28; matrix products, arithmetic and copies ran while one was open for 1% -> 1% of each run, Pallas kernels for 17% -> 19%
where the time goes in v1:
time: 294 us; the launch traced here: 293 us
  waiting for transfers between devices  104 us (35%)
  starting transfers between devices  96.3 us (33%)
  Pallas kernels  65.3 us (22%)
  local copies, waits for them, and re-layouts  25.2 us (9%)
    ppermute x36, waiting for transfers between devices, to_peer(): return lax.ppermute(value, 'pts', [(i, i ^ o) for i in range(n_pts)])  71.8 us
    ppermute x36, starting transfers between devices, to_peer(): return lax.ppermute(value, 'pts', [(i, i ^ o) for i in range(n_pts)])  43.9 us
    ppermute x28, starting transfers between devices, across(): lax.ppermute(value, 'mat', [(i, i ^ d) for i in range(n_mat)])  32.9 us
    ppermute x28, waiting for transfers between devices, across(): lax.ppermute(value, 'mat', [(i, i ^ d) for i in range(n_mat)])  32 us
    unnamed x40, local copies, waits for them, and re-layouts  21.7 us
    pallas_call x6, Pallas kernels, response(): pl.pallas_call(functools.partial(response_kernel, dims, start, rows, 256)...  20.9 us
    pallas_call x5, Pallas kernels, density(): pl.pallas_call(functools.partial(density_kernel, dims, start, rows, 256),...  19.8 us
    all_to_all x4, starting transfers between devices, across(): return lax.all_to_all(values, 'mat', 0, 0, tiled=True)  19.5 us
  transfers between devices with their start and end apart: 68, of which 28 were waited for; matrix products, arithmetic and copies ran while one was open for 1% of the time, Pallas kernels for 19%

profile of v1, /device:TPU:0, one launch (start us, length us, event | category | flops | bytes accessed | tf_op | source)
XLA Modules:
  0.0 292.8 jit_solution(13656988988175888959)
XLA Ops:
  3.1 6.4 %all-to-all-start = ((bf16[8,256,256]{2,1,0:T(8,128)(2,1)}), bf16[8,256,256]{2,1,0:T(8,128)(2,1)S(1)}, u32[]{:S(2)}, u32[]{:S(2)}) async-start(bf16[8,256,256]{2,1,0:T(8,128)(2,1)} %slice.3), calls=%async_computation | async-start | bytes 2097152 | tf_op jit(solution)/shard_map/all_to_all | solution.py:292
  10.4 3.5 %collective-permute-start.28 = (bf16[128,256]{1,0:T(8,128)(2,1)}, bf16[128,256]{1,0:T(8,128)(2,1)S(1)}, u32[]{:S(2)}, u32[]{:S(2)}) collective-permute-start(bf16[128,256]{1,0:T(8,128)(2,1)} %get-tuple-element.122), channel_id=1, source_target_pairs={{0,28},{4,24},{8,20},{12,16},{16,12},{20,8},{24,4},{28,0},{1,29},{... | collective-permute-start | bytes 196616 | tf_op jit(solution)/shard_map/ppermute | solution.py:294
  21.7 10.6 %collective-permute-done.28.refs_7_ = bf16[128,256]{1,0:T(8,128)(2,1)S(1)} collective-permute-done((bf16[128,256]{1,0:T(8,128)(2,1)}, bf16[128,256]{1,0:T(8,128)(2,1)S(1)}, u32[]{:S(2)}, u32[]{:S(2)}) %collective-permute-start.28) | collective-permute-done | bytes 65568 | tf_op jit(solution)/shard_map/ppermute | solution.py:294
  33.2 9.2 %collective-permute-done.26.refs_5_ = bf16[128,256]{1,0:T(8,128)(2,1)S(1)} collective-permute-done((bf16[128,256]{1,0:T(8,128)(2,1)}, bf16[128,256]{1,0:T(8,128)(2,1)S(1)}, u32[]{:S(2)}, u32[]{:S(2)}) %collective-permute-start.26) | collective-permute-done | bytes 65568 | tf_op jit(solution)/shard_map/ppermute | solution.py:294
  44.5 5.0 %collective-permute-done.27.refs_6_ = bf16[128,256]{1,0:T(8,128)(2,1)S(1)} collective-permute-done((bf16[128,256]{1,0:T(8,128)(2,1)}, bf16[128,256]{1,0:T(8,128)(2,1)S(1)}, u32[]{:S(2)}, u32[]{:S(2)}) %collective-permute-start.27) | collective-permute-done | bytes 65568 | tf_op jit(solution)/shard_map/ppermute | solution.py:294
  52.1 3.3 %collective-permute-start.17 = (bf16[128,256]{1,0:T(8,128)(2,1)}, bf16[128,256]{1,0:T(8,128)(2,1)S(1)}, u32[]{:S(2)}, u32[]{:S(2)}) collective-permute-start(bf16[128,256]{1,0:T(8,128)(2,1)} %get-tuple-element.130), channel_id=1, source_target_pairs={{0,24},{4,28},{8,16},{12,20},{16,8},{20,12},{24,0},{28,4},{1,25},{... | collective-permute-start | bytes 196616 | tf_op jit(solution)/shard_map/ppermute | solution.py:294
  60.3 3.9 %collective-permute-done.16.refs_5_ = bf16[128,256]{1,0:T(8,128)(2,1)S(1)} collective-permute-done((bf16[128,256]{1,0:T(8,128)(2,1)}, bf16[128,256]{1,0:T(8,128)(2,1)S(1)}, u32[]{:S(2)}, u32[]{:S(2)}) %collective-permute-start.16) | collective-permute-done | bytes 65568 | tf_op jit(solution)/shard_map/ppermute | solution.py:294
  81.5 4.5 %collective-permute-done.30.refs_2_ = bf16[128,1536]{1,0:T(8,128)(2,1)S(1)} collective-permute-done((bf16[128,1536]{1,0:T(8,128)(2,1)S(1)}, bf16[128,1536]{1,0:T(8,128)(2,1)S(1)}, u32[]{:S(2)}, u32[]{:S(2)}) %collective-permute-start.30) | collective-permute-done | bytes 393248 | tf_op jit(solution)/shard_map/ppermute | solution.py:284
  92.5 4.8 %shard_map.100.refs_5_ = f32[1,1536]{1,0:T(1,128)S(1)} custom-call(s32[307]{0:T(512)S(1)} %concatenate.3.meta, bf16[128,1536]{1,0:T(8,128)(2,1)S(1)} %get-tuple-element.78.refs_0_, bf16[128,1536]{1,0:T(8,128)(2,1)S(1)} %collective-permute-done.29.refs_1_, bf16[128,1536]{1,0:T(8,128)(2,1)S(1)} %collective-permute-done.30.refs_2_, ...), custom_call_target="tpu_custom_call" | custom-call | flops 2415919104 | bytes 4718592 | tf_op jit(solution)/shard_map/pallas_call | solution.py:127
  98.3 4.8 %collective-permute-done.20.refs_2_ = bf16[128,1536]{1,0:T(8,128)(2,1)} collective-permute-done((bf16[128,1536]{1,0:T(8,128)(2,1)}, bf16[128,1536]{1,0:T(8,128)(2,1)}, u32[]{:S(2)}, u32[]{:S(2)}) %collective-permute-start.20) | collective-permute-done | bytes 393248 | tf_op jit(solution)/shard_map/ppermute | solution.py:284
  103.6 4.9 %shard_map.101.refs_5_ = f32[1,1536]{1,0:T(1,128)S(1)} custom-call(s32[307]{0:T(512)S(1)} %concatenate.3.meta, bf16[128,1536]{1,0:T(8,128)(2,1)S(1)} %copy-done.15, bf16[128,1536]{1,0:T(8,128)(2,1)} %collective-permute-done.19.refs_1_, bf16[128,1536]{1,0:T(8,128)(2,1)} %collective-permute-done.20.refs_2_, bf16[128,1536]{1,0:T(8,128)(2,1)} %collective-permute-done.21.refs_3_, ...), custom_call_target="tpu_custom_call" | custom-call | flops 2415919104 | bytes 4718592 | tf_op jit(solution)/shard_map/pallas_call | solution.py:127
  112.0 3.9 %collective-permute-done.6.refs_1_ = bf16[64,1536]{1,0:T(8,128)(2,1)S(1)} collective-permute-done((bf16[64,1536]{1,0:T(8,128)(2,1)S(1)}, bf16[64,1536]{1,0:T(8,128)(2,1)S(1)}, u32[]{:S(2)}, u32[]{:S(2)}) %collective-permute-start.6) | collective-permute-done | bytes 196640 | tf_op jit(solution)/shard_map/ppermute | solution.py:284
  118.9 4.5 %collective-permute-done.10.refs_2_ = bf16[128,1536]{1,0:T(8,128)(2,1)S(1)} collective-permute-done((bf16[128,1536]{1,0:T(8,128)(2,1)S(1)}, bf16[128,1536]{1,0:T(8,128)(2,1)S(1)}, u32[]{:S(2)}, u32[]{:S(2)}) %collective-permute-start.10) | collective-permute-done | bytes 393248 | tf_op jit(solution)/shard_map/ppermute | solution.py:284
  125.4 4.2 %shard_map.102.refs_5_ = f32[1,1536]{1,0:T(1,128)S(1)} custom-call(s32[307]{0:T(512)S(1)} %concatenate.3.meta, bf16[128,1536]{1,0:T(8,128)(2,1)S(1)} %get-tuple-element.70.refs_0_, bf16[128,1536]{1,0:T(8,128)(2,1)S(1)} %collective-permute-done.9.refs_1_, bf16[128,1536]{1,0:T(8,128)(2,1)S(1)} %collective-permute-done.10.refs_2_, ...), custom_call_target="tpu_custom_call" | custom-call | flops 2415919104 | bytes 4718592 | tf_op jit(solution)/shard_map/pallas_call | solution.py:127
  132.4 3.0 %shard_map.103.refs_5_ = f32[1,1536]{1,0:T(1,128)S(1)} custom-call(s32[307]{0:T(512)S(1)} %concatenate.3.meta, bf16[64,1536]{1,0:T(8,128)(2,1)S(1)} %get-tuple-element.66.refs_0_, bf16[64,1536]{1,0:T(8,128)(2,1)S(1)} %collective-permute-done.6.refs_1_, bf16[64,1536]{1,0:T(8,128)(2,1)S(1)} %collective-permute-done.7.refs_2_, ...), custom_call_target="tpu_custom_call" | custom-call | flops 1207959552 | bytes 4718592 | tf_op jit(solution)/shard_map/pallas_call | solution.py:127
  135.7 3.0 %shard_map.104.refs_2_ = f32[1,1536]{1,0:T(1,128)S(1)} custom-call(s32[307]{0:T(512)S(1)} %concatenate.3.meta, bf16[64,1536]{1,0:T(8,128)(2,1)S(1)} %get-tuple-element.62.refs_0_, bf16[64,1536]{1,0:T(8,128)(2,1)S(1)} %collective-permute-done.3.refs_1_, bf16[64,1536]{1,0:T(8,128)(2,1)S(1)} %collective-permute-done.4.refs_2_, ...), custom_call_target="tpu_custom_call" | custom-call | flops 1207959552 | bytes 4718592 | tf_op jit(solution)/shard_map/pallas_call | solution.py:127
  138.7 3.0 %shard_map.114 = (bf16[64,1536]{1,0:T(8,128)(2,1)S(1)}, bf16[64,1536]{1,0:T(8,128)(2,1)S(1)}, bf16[64,1536]{1,0:T(8,128)(2,1)S(1)}, bf16[64,1536]{1,0:T(8,128)(2,1)S(1)}) custom-call(s32[307]{0:T(512)S(1)} %concatenate.3.meta, bf16[1536,1536]{1,0:T(8,128)(2,1)S(1)} %copy-done.3, bf16[1536,1536]{1,0:T(8,128)(2,1)S(1)} %bitcast.43, ...), custom_call_target="tpu_custom_call" | custom-call | flops 1207959552 | bytes 9437184 | tf_op jit(solution)/shard_map/pallas_call | solution.py:163
  145.3 3.0 %shard_map.113 = (bf16[64,1536]{1,0:T(8,128)(2,1)S(1)}, bf16[64,1536]{1,0:T(8,128)(2,1)S(1)}, bf16[64,1536]{1,0:T(8,128)(2,1)S(1)}, bf16[64,1536]{1,0:T(8,128)(2,1)S(1)}) custom-call(s32[307]{0:T(512)S(1)} %concatenate.3.meta, bf16[1536,1536]{1,0:T(8,128)(2,1)S(1)} %copy-done.3, bf16[1536,1536]{1,0:T(8,128)(2,1)S(1)} %bitcast.44, ...), custom_call_target="tpu_custom_call" | custom-call | flops 1207959552 | bytes 9437184 | tf_op jit(solution)/shard_map/pallas_call | solution.py:163
  154.7 3.3 %collective-permute-done.58.refs_1_ = bf16[64,1536]{1,0:T(8,128)(2,1)S(1)} collective-permute-done((bf16[64,1536]{1,0:T(8,128)(2,1)S(1)}, bf16[64,1536]{1,0:T(8,128)(2,1)S(1)}, u32[]{:S(2)}, u32[]{:S(2)}) %collective-permute-start.58) | collective-permute-done | bytes 196640 | tf_op jit(solution)/shard_map/ppermute | solution.py:284
  163.7 3.7 %all-to-all-start.3 = ((bf16[8,128,256]{2,1,0:T(8,128)(2,1)}), bf16[8,128,256]{2,1,0:T(8,128)(2,1)S(1)}, u32[]{:S(2)}, u32[]{:S(2)}) async-start(bf16[8,128,256]{2,1,0:T(8,128)(2,1)} %shard_map.115), calls=%async_computation.3 | async-start | bytes 1048576 | tf_op jit(solution)/shard_map/all_to_all | solution.py:292
  172.0 4.4 %shard_map.111 = (bf16[128,1536]{1,0:T(8,128)(2,1)S(1)}, bf16[128,1536]{1,0:T(8,128)(2,1)S(1)}, bf16[128,1536]{1,0:T(8,128)(2,1)S(1)}, bf16[128,1536]{1,0:T(8,128)(2,1)S(1)}) custom-call(s32[307]{0:T(512)S(1)} %concatenate.3.meta, bf16[1536,1536]{1,0:T(8,128)(2,1)S(1)} %copy-done.4, bf16[1536,1536]{1,0:T(8,128)(2,1)S(1)} %bitcast.45, ...), custom_call_target="tpu_custom_call" | custom-call | flops 2415919104 | bytes 9437184 | tf_op jit(solution)/shard_map/pallas_call | solution.py:163
  180.0 8.5 %collective-permute-done.55.refs_1_ = bf16[128,1536]{1,0:T(8,128)(2,1)S(1)} collective-permute-done((bf16[128,1536]{1,0:T(8,128)(2,1)S(1)}, bf16[128,1536]{1,0:T(8,128)(2,1)S(1)}, u32[]{:S(2)}, u32[]{:S(2)}) %collective-permute-start.55) | collective-permute-done | bytes 393248 | tf_op jit(solution)/shard_map/ppermute | solution.py:284
  188.5 8.2 %collective-permute-done.56.refs_2_ = bf16[128,1536]{1,0:T(8,128)(2,1)S(1)} collective-permute-done((bf16[128,1536]{1,0:T(8,128)(2,1)S(1)}, bf16[128,1536]{1,0:T(8,128)(2,1)S(1)}, u32[]{:S(2)}, u32[]{:S(2)}) %collective-permute-start.56) | collective-permute-done | bytes 393248 | tf_op jit(solution)/shard_map/ppermute | solution.py:284
  198.8 4.7 %all-to-all-start.2 = ((bf16[8,128,256]{2,1,0:T(8,128)(2,1)}), bf16[8,128,256]{2,1,0:T(8,128)(2,1)S(1)}, u32[]{:S(2)}, u32[]{:S(2)}) async-start(bf16[8,128,256]{2,1,0:T(8,128)(2,1)} %shard_map.112), calls=%async_computation.2 | async-start | bytes 1048576 | tf_op jit(solution)/shard_map/all_to_all | solution.py:292
  208.2 4.4 %shard_map.109 = (bf16[128,1536]{1,0:T(8,128)(2,1)S(1)}, bf16[128,1536]{1,0:T(8,128)(2,1)S(1)}, bf16[128,1536]{1,0:T(8,128)(2,1)S(1)}, bf16[128,1536]{1,0:T(8,128)(2,1)S(1)}) custom-call(s32[307]{0:T(512)S(1)} %concatenate.3.meta, bf16[1536,1536]{1,0:T(8,128)(2,1)S(1)} %copy-done.5, bf16[1536,1536]{1,0:T(8,128)(2,1)S(1)} %bitcast.46, ...), custom_call_target="tpu_custom_call" | custom-call | flops 2415919104 | bytes 9437184 | tf_op jit(solution)/shard_map/pallas_call | solution.py:163
  216.2 8.5 %collective-permute-done.52.refs_1_ = bf16[128,1536]{1,0:T(8,128)(2,1)S(1)} collective-permute-done((bf16[128,1536]{1,0:T(8,128)(2,1)S(1)}, bf16[128,1536]{1,0:T(8,128)(2,1)S(1)}, u32[]{:S(2)}, u32[]{:S(2)}) %collective-permute-start.52) | collective-permute-done | bytes 393248 | tf_op jit(solution)/shard_map/ppermute | solution.py:284
  224.7 7.3 %collective-permute-done.53.refs_2_ = bf16[128,1536]{1,0:T(8,128)(2,1)S(1)} collective-permute-done((bf16[128,1536]{1,0:T(8,128)(2,1)S(1)}, bf16[128,1536]{1,0:T(8,128)(2,1)S(1)}, u32[]{:S(2)}, u32[]{:S(2)}) %collective-permute-start.53) | collective-permute-done | bytes 393248 | tf_op jit(solution)/shard_map/ppermute | solution.py:284
  235.8 4.7 %all-to-all-start.1 = ((bf16[8,128,256]{2,1,0:T(8,128)(2,1)}), bf16[8,128,256]{2,1,0:T(8,128)(2,1)S(1)}, u32[]{:S(2)}, u32[]{:S(2)}) async-start(bf16[8,128,256]{2,1,0:T(8,128)(2,1)} %shard_map.110), calls=%async_computation.1 | async-start | bytes 1048576 | tf_op jit(solution)/shard_map/all_to_all | solution.py:292
  245.1 3.0 %shard_map.107 = (bf16[64,1536]{1,0:T(8,128)(2,1)S(1)}, bf16[64,1536]{1,0:T(8,128)(2,1)S(1)}, bf16[64,1536]{1,0:T(8,128)(2,1)S(1)}, bf16[64,1536]{1,0:T(8,128)(2,1)S(1)}) custom-call(s32[307]{0:T(512)S(1)} %concatenate.3.meta, bf16[1536,1536]{1,0:T(8,128)(2,1)S(1)} %copy-done.6, bf16[1536,1536]{1,0:T(8,128)(2,1)S(1)} %bitcast.47, ...), custom_call_target="tpu_custom_call" | custom-call | flops 1207959552 | bytes 9437184 | tf_op jit(solution)/shard_map/pallas_call | solution.py:163
  251.7 3.0 %shard_map.105 = (bf16[64,1536]{1,0:T(8,128)(2,1)S(1)}, bf16[64,1536]{1,0:T(8,128)(2,1)S(1)}, bf16[64,1536]{1,0:T(8,128)(2,1)S(1)}, bf16[64,1536]{1,0:T(8,128)(2,1)S(1)}) custom-call(s32[307]{0:T(512)S(1)} %concatenate.3.meta, bf16[1536,1536]{1,0:T(8,128)(2,1)S(1)} %copy-done.6, bf16[1536,1536]{1,0:T(8,128)(2,1)S(1)} %bitcast.48, ...), custom_call_target="tpu_custom_call" | custom-call | flops 1207959552 | bytes 9437184 | tf_op jit(solution)/shard_map/pallas_call | solution.py:163
  264.5 4.2 %collective-permute-done.33.refs_2_ = bf16[64,1536]{1,0:T(8,128)(2,1)S(1)} collective-permute-done((bf16[64,1536]{1,0:T(8,128)(2,1)S(1)}, bf16[64,1536]{1,0:T(8,128)(2,1)S(1)}, u32[]{:S(2)}, u32[]{:S(2)}) %collective-permute-start.33) | collective-permute-done | bytes 196640 | tf_op jit(solution)/shard_map/ppermute | solution.py:284
  280.8 3.2 %collective-permute-start.40 = (bf16[64,256]{1,0:T(8,128)(2,1)S(1)}, bf16[64,256]{1,0:T(8,128)(2,1)S(1)}, u32[]{:S(2)}, u32[]{:S(2)}) collective-permute-start(bf16[64,256]{1,0:T(8,128)(2,1)S(1)} %get-tuple-element.92), channel_id=1, source_target_pairs={{0,24},{4,28},{8,16},{12,20},{16,8},{20,12},{24,0},{28,4},{1,25},{... | collective-permute-start | bytes 98312 | tf_op jit(solution)/shard_map/ppermute | solution.py:294
  (179 shorter events, 134.5 us)
Async XLA Ops:
  3.1 77.3 %all-to-all-start = ((bf16[8,256,256]{2,1,0:T(8,128)(2,1)}), bf16[8,256,256]{2,1,0:T(8,128)(2,1)S(1)}, u32[]{:S(2)}, u32[]{:S(2)}) async-start(bf16[8,256,256]{2,1,0:T(8,128)(2,1)} %slice.3), calls=%async_computation | async-start | bytes 2097152 | tf_op jit(solution)/shard_map/all_to_all | solution.py:292
  10.4 21.9 %collective-permute-start.28 = (bf16[128,256]{1,0:T(8,128)(2,1)}, bf16[128,256]{1,0:T(8,128)(2,1)S(1)}, u32[]{:S(2)}, u32[]{:S(2)}) collective-permute-start(bf16[128,256]{1,0:T(8,128)(2,1)} %get-tuple-element.122), channel_id=1, source_target_pairs={{0,28},{4,24},{8,20},{12,16},{16,12},{20,8},{24,4},{28,0},{1,29},{... | collective-permute-start | bytes 196616 | tf_op jit(solution)/shard_map/ppermute | solution.py:294
  13.9 28.6 %collective-permute-start.26 = (bf16[128,256]{1,0:T(8,128)(2,1)}, bf16[128,256]{1,0:T(8,128)(2,1)S(1)}, u32[]{:S(2)}, u32[]{:S(2)}) collective-permute-start(bf16[128,256]{1,0:T(8,128)(2,1)} %get-tuple-element.123), channel_id=1, source_target_pairs={{0,20},{4,16},{8,28},{12,24},{16,4},{20,0},{24,12},{28,8},{1,21},{... | collective-permute-start | bytes 196616 | tf_op jit(solution)/shard_map/ppermute | solution.py:294
  18.4 26.1 %collective-permute-start.25 = (bf16[128,256]{1,0:T(8,128)(2,1)}, bf16[128,256]{1,0:T(8,128)(2,1)S(1)}, u32[]{:S(2)}, u32[]{:S(2)}) collective-permute-start(bf16[128,256]{1,0:T(8,128)(2,1)} %get-tuple-element.124), channel_id=1, source_target_pairs={{0,16},{4,20},{8,24},{12,28},{16,0},{20,4},{24,8},{28,12},{1,17},{... | collective-permute-start | bytes 196616 | tf_op jit(solution)/shard_map/ppermute | solution.py:294
  21.3 23.2 %collective-permute-start.24 = (bf16[128,256]{1,0:T(8,128)(2,1)}, bf16[128,256]{1,0:T(8,128)(2,1)S(1)}, u32[]{:S(2)}, u32[]{:S(2)}) collective-permute-start(bf16[128,256]{1,0:T(8,128)(2,1)} %get-tuple-element.125), channel_id=1, source_target_pairs={{0,12},{4,8},{8,4},{12,0},{16,28},{20,24},{24,20},{28,16},{1,13},{... | collective-permute-start | bytes 196616 | tf_op jit(solution)/shard_map/ppermute | solution.py:294
  21.3 23.2 %collective-permute-start.23 = (bf16[128,256]{1,0:T(8,128)(2,1)}, bf16[128,256]{1,0:T(8,128)(2,1)S(1)}, u32[]{:S(2)}, u32[]{:S(2)}) collective-permute-start(bf16[128,256]{1,0:T(8,128)(2,1)} %get-tuple-element.126), channel_id=1, source_target_pairs={{0,8},{4,12},{8,0},{12,4},{16,24},{20,28},{24,16},{28,20},{1,9},{5... | collective-permute-start | bytes 196616 | tf_op jit(solution)/shard_map/ppermute | solution.py:294
  32.3 12.2 %collective-permute-start.22 = (bf16[128,256]{1,0:T(8,128)(2,1)}, bf16[128,256]{1,0:T(8,128)(2,1)S(1)}, u32[]{:S(2)}, u32[]{:S(2)}) collective-permute-start(bf16[128,256]{1,0:T(8,128)(2,1)} %get-tuple-element.127), channel_id=1, source_target_pairs={{0,4},{4,0},{8,12},{12,8},{16,20},{20,16},{24,28},{28,24},{1,5},{5... | collective-permute-start | bytes 196616 | tf_op jit(solution)/shard_map/ppermute | solution.py:294
  50.6 22.9 %collective-permute-start.29 = (bf16[128,1536]{1,0:T(8,128)(2,1)S(1)}, bf16[128,1536]{1,0:T(8,128)(2,1)S(1)}, u32[]{:S(2)}, u32[]{:S(2)}) collective-permute-start(bf16[128,1536]{1,0:T(8,128)(2,1)S(1)} %get-tuple-element.79), channel_id=1, source_target_pairs={{0,1},{1,0},{2,3},{3,2},{4,5},{5,4},{6,7},{7,6},{8,9},{9,8},{10,11... | collective-permute-start | bytes 1179656 | tf_op jit(solution)/shard_map/ppermute | solution.py:284
  65.7 20.4 %collective-permute-start.30 = (bf16[128,1536]{1,0:T(8,128)(2,1)S(1)}, bf16[128,1536]{1,0:T(8,128)(2,1)S(1)}, u32[]{:S(2)}, u32[]{:S(2)}) collective-permute-start(bf16[128,1536]{1,0:T(8,128)(2,1)S(1)} %get-tuple-element.80), channel_id=1, source_target_pairs={{0,2},{1,3},{2,0},{3,1},{4,6},{5,7},{6,4},{7,5},{8,10},{9,11},{10,... | collective-permute-start | bytes 1179656 | tf_op jit(solution)/shard_map/ppermute | solution.py:284
  67.2 19.4 %collective-permute-start.31 = (bf16[128,1536]{1,0:T(8,128)(2,1)S(1)}, bf16[128,1536]{1,0:T(8,128)(2,1)}, u32[]{:S(2)}, u32[]{:S(2)}) collective-permute-start(bf16[128,1536]{1,0:T(8,128)(2,1)S(1)} %get-tuple-element.81), channel_id=1, source_target_pairs={{0,3},{1,2},{2,1},{3,0},{4,7},{5,6},{6,5},{7,4},{8,11},{9,10},{10,... | collective-permute-start | bytes 1179656 | tf_op jit(solution)/shard_map/ppermute | solution.py:284
  70.5 18.7 %collective-permute-start.19 = (bf16[128,1536]{1,0:T(8,128)(2,1)}, bf16[128,1536]{1,0:T(8,128)(2,1)}, u32[]{:S(2)}, u32[]{:S(2)}) collective-permute-start(bf16[128,1536]{1,0:T(8,128)(2,1)} %get-tuple-element.75), channel_id=1, source_target_pairs={{0,1},{1,0},{2,3},{3,2},{4,5},{5,4},{6,7},{7,6},{8,9},{9,8},{10,11... | collective-permute-start | bytes 1179656 | tf_op jit(solution)/shard_map/ppermute | solution.py:284
  71.9 31.1 %collective-permute-start.20 = (bf16[128,1536]{1,0:T(8,128)(2,1)}, bf16[128,1536]{1,0:T(8,128)(2,1)}, u32[]{:S(2)}, u32[]{:S(2)}) collective-permute-start(bf16[128,1536]{1,0:T(8,128)(2,1)} %get-tuple-element.76), channel_id=1, source_target_pairs={{0,2},{1,3},{2,0},{3,1},{4,6},{5,7},{6,4},{7,5},{8,10},{9,11},{10,... | collective-permute-start | bytes 1179656 | tf_op jit(solution)/shard_map/ppermute | solution.py:284
  73.5 30.1 %collective-permute-start.21 = (bf16[128,1536]{1,0:T(8,128)(2,1)}, bf16[128,1536]{1,0:T(8,128)(2,1)}, u32[]{:S(2)}, u32[]{:S(2)}) collective-permute-start(bf16[128,1536]{1,0:T(8,128)(2,1)} %get-tuple-element.77), channel_id=1, source_target_pairs={{0,3},{1,2},{2,1},{3,0},{4,7},{5,6},{6,5},{7,4},{8,11},{9,10},{10,... | collective-permute-start | bytes 1179656 | tf_op jit(solution)/shard_map/ppermute | solution.py:284
  86.1 31.3 %collective-permute-start.9 = (bf16[128,1536]{1,0:T(8,128)(2,1)S(1)}, bf16[128,1536]{1,0:T(8,128)(2,1)S(1)}, u32[]{:S(2)}, u32[]{:S(2)}) collective-permute-start(bf16[128,1536]{1,0:T(8,128)(2,1)S(1)} %get-tuple-element.71), channel_id=1, source_target_pairs={{0,1},{1,0},{2,3},{3,2},{4,5},{5,4},{6,7},{7,6},{8,9},{9,8},{10,11... | collective-permute-start | bytes 1179656 | tf_op jit(solution)/shard_map/ppermute | solution.py:284
  86.6 36.8 %collective-permute-start.10 = (bf16[128,1536]{1,0:T(8,128)(2,1)S(1)}, bf16[128,1536]{1,0:T(8,128)(2,1)S(1)}, u32[]{:S(2)}, u32[]{:S(2)}) collective-permute-start(bf16[128,1536]{1,0:T(8,128)(2,1)S(1)} %get-tuple-element.72), channel_id=1, source_target_pairs={{0,2},{1,3},{2,0},{3,1},{4,6},{5,7},{6,4},{7,5},{8,10},{9,11},{10,... | collective-permute-start | bytes 1179656 | tf_op jit(solution)/shard_map/ppermute | solution.py:284
  89.1 35.8 %collective-permute-start.11 = (bf16[128,1536]{1,0:T(8,128)(2,1)S(1)}, bf16[128,1536]{1,0:T(8,128)(2,1)S(1)}, u32[]{:S(2)}, u32[]{:S(2)}) collective-permute-start(bf16[128,1536]{1,0:T(8,128)(2,1)S(1)} %get-tuple-element.73), channel_id=1, source_target_pairs={{0,3},{1,2},{2,1},{3,0},{4,7},{5,6},{6,5},{7,4},{8,11},{9,10},{10,... | collective-permute-start | bytes 1179656 | tf_op jit(solution)/shard_map/ppermute | solution.py:284
  103.0 12.9 %collective-permute-start.6 = (bf16[64,1536]{1,0:T(8,128)(2,1)S(1)}, bf16[64,1536]{1,0:T(8,128)(2,1)S(1)}, u32[]{:S(2)}, u32[]{:S(2)}) collective-permute-start(bf16[64,1536]{1,0:T(8,128)(2,1)S(1)} %get-tuple-element.67), channel_id=1, source_target_pairs={{0,1},{1,0},{2,3},{3,2},{4,5},{5,4},{6,7},{7,6},{8,9},{9,8},{10,11... | collective-permute-start | bytes 589832 | tf_op jit(solution)/shard_map/ppermute | solution.py:284
  108.5 23.9 %collective-permute-start.7 = (bf16[64,1536]{1,0:T(8,128)(2,1)S(1)}, bf16[64,1536]{1,0:T(8,128)(2,1)S(1)}, u32[]{:S(2)}, u32[]{:S(2)}) collective-permute-start(bf16[64,1536]{1,0:T(8,128)(2,1)S(1)} %get-tuple-element.68), channel_id=1, source_target_pairs={{0,2},{1,3},{2,0},{3,1},{4,6},{5,7},{6,4},{7,5},{8,10},{9,11},{10,... | collective-permute-start | bytes 589832 | tf_op jit(solution)/shard_map/ppermute | solution.py:284
  115.9 16.5 %collective-permute-start.8 = (bf16[64,1536]{1,0:T(8,128)(2,1)S(1)}, bf16[64,1536]{1,0:T(8,128)(2,1)S(1)}, u32[]{:S(2)}, u32[]{:S(2)}) collective-permute-start(bf16[64,1536]{1,0:T(8,128)(2,1)S(1)} %get-tuple-element.69), channel_id=1, source_target_pairs={{0,3},{1,2},{2,1},{3,0},{4,7},{5,6},{6,5},{7,4},{8,11},{9,10},{10,... | collective-permute-start | bytes 589832 | tf_op jit(solution)/shard_map/ppermute | solution.py:284
  117.4 18.0 %collective-permute-start.3 = (bf16[64,1536]{1,0:T(8,128)(2,1)S(1)}, bf16[64,1536]{1,0:T(8,128)(2,1)S(1)}, u32[]{:S(2)}, u32[]{:S(2)}) collective-permute-start(bf16[64,1536]{1,0:T(8,128)(2,1)S(1)} %get-tuple-element.63), channel_id=1, source_target_pairs={{0,1},{1,0},{2,3},{3,2},{4,5},{5,4},{6,7},{7,6},{8,9},{9,8},{10,11... | collective-permute-start | bytes 589832 | tf_op jit(solution)/shard_map/ppermute | solution.py:284
  123.4 12.3 %collective-permute-start.4 = (bf16[64,1536]{1,0:T(8,128)(2,1)S(1)}, bf16[64,1536]{1,0:T(8,128)(2,1)S(1)}, u32[]{:S(2)}, u32[]{:S(2)}) collective-permute-start(bf16[64,1536]{1,0:T(8,128)(2,1)S(1)} %get-tuple-element.64), channel_id=1, source_target_pairs={{0,2},{1,3},{2,0},{3,1},{4,6},{5,7},{6,4},{7,5},{8,10},{9,11},{10,... | collective-permute-start | bytes 589832 | tf_op jit(solution)/shard_map/ppermute | solution.py:284
  163.7 35.1 %all-to-all-start.3 = ((bf16[8,128,256]{2,1,0:T(8,128)(2,1)}), bf16[8,128,256]{2,1,0:T(8,128)(2,1)S(1)}, u32[]{:S(2)}, u32[]{:S(2)}) async-start(bf16[8,128,256]{2,1,0:T(8,128)(2,1)} %shard_map.115), calls=%async_computation.3 | async-start | bytes 1048576 | tf_op jit(solution)/shard_map/all_to_all | solution.py:292
  177.3 19.4 %collective-permute-start.56 = (bf16[128,1536]{1,0:T(8,128)(2,1)S(1)}, bf16[128,1536]{1,0:T(8,128)(2,1)S(1)}, u32[]{:S(2)}, u32[]{:S(2)}) collective-permute-start(bf16[128,1536]{1,0:T(8,128)(2,1)S(1)} %get-tuple-element.112), channel_id=1, source_target_pairs={{0,2},{1,3},{2,0},{3,1},{4,6},{5,7},{6,4},{7,5},{8,10},{9,11},{10,... | collective-permute-start | bytes 1179656 | tf_op jit(solution)/shard_map/ppermute | solution.py:284
  178.8 17.9 %collective-permute-start.57 = (bf16[128,1536]{1,0:T(8,128)(2,1)S(1)}, bf16[128,1536]{1,0:T(8,128)(2,1)S(1)}, u32[]{:S(2)}, u32[]{:S(2)}) collective-permute-start(bf16[128,1536]{1,0:T(8,128)(2,1)S(1)} %get-tuple-element.113), channel_id=1, source_target_pairs={{0,3},{1,2},{2,1},{3,0},{4,7},{5,6},{6,5},{7,4},{8,11},{9,10},{10,... | collective-permute-start | bytes 1179656 | tf_op jit(solution)/shard_map/ppermute | solution.py:284
  198.8 36.9 %all-to-all-start.2 = ((bf16[8,128,256]{2,1,0:T(8,128)(2,1)}), bf16[8,128,256]{2,1,0:T(8,128)(2,1)S(1)}, u32[]{:S(2)}, u32[]{:S(2)}) async-start(bf16[8,128,256]{2,1,0:T(8,128)(2,1)} %shard_map.112), calls=%async_computation.2 | async-start | bytes 1048576 | tf_op jit(solution)/shard_map/all_to_all | solution.py:292
  214.0 18.0 %collective-permute-start.53 = (bf16[128,1536]{1,0:T(8,128)(2,1)S(1)}, bf16[128,1536]{1,0:T(8,128)(2,1)S(1)}, u32[]{:S(2)}, u32[]{:S(2)}) collective-permute-start(bf16[128,1536]{1,0:T(8,128)(2,1)S(1)} %get-tuple-element.108), channel_id=1, source_target_pairs={{0,2},{1,3},{2,0},{3,1},{4,6},{5,7},{6,4},{7,5},{8,10},{9,11},{10,... | collective-permute-start | bytes 1179656 | tf_op jit(solution)/shard_map/ppermute | solution.py:284
  214.8 18.9 %collective-permute-start.54 = (bf16[128,1536]{1,0:T(8,128)(2,1)S(1)}, bf16[128,1536]{1,0:T(8,128)(2,1)S(1)}, u32[]{:S(2)}, u32[]{:S(2)}) collective-permute-start(bf16[128,1536]{1,0:T(8,128)(2,1)S(1)} %get-tuple-element.109), channel_id=1, source_target_pairs={{0,3},{1,2},{2,1},{3,0},{4,7},{5,6},{6,5},{7,4},{8,11},{9,10},{10,... | collective-permute-start | bytes 1179656 | tf_op jit(solution)/shard_map/ppermute | solution.py:284
  235.8 52.6 %all-to-all-start.1 = ((bf16[8,128,256]{2,1,0:T(8,128)(2,1)}), bf16[8,128,256]{2,1,0:T(8,128)(2,1)S(1)}, u32[]{:S(2)}, u32[]{:S(2)}) async-start(bf16[8,128,256]{2,1,0:T(8,128)(2,1)} %shard_map.110), calls=%async_computation.1 | async-start | bytes 1048576 | tf_op jit(solution)/shard_map/all_to_all | solution.py:292
  255.6 13.1 %collective-permute-start.33 = (bf16[64,1536]{1,0:T(8,128)(2,1)S(1)}, bf16[64,1536]{1,0:T(8,128)(2,1)S(1)}, u32[]{:S(2)}, u32[]{:S(2)}) collective-permute-start(bf16[64,1536]{1,0:T(8,128)(2,1)S(1)} %get-tuple-element.84), channel_id=1, source_target_pairs={{0,2},{1,3},{2,0},{3,1},{4,6},{5,7},{6,4},{7,5},{8,10},{9,11},{10,... | collective-permute-start | bytes 589832 | tf_op jit(solution)/shard_map/ppermute | solution.py:284
  257.1 14.1 %collective-permute-start.34 = (bf16[64,1536]{1,0:T(8,128)(2,1)S(1)}, bf16[64,1536]{1,0:T(8,128)(2,1)S(1)}, u32[]{:S(2)}, u32[]{:S(2)}) collective-permute-start(bf16[64,1536]{1,0:T(8,128)(2,1)S(1)} %get-tuple-element.85), channel_id=1, source_target_pairs={{0,3},{1,2},{2,1},{3,0},{4,7},{5,6},{6,5},{7,4},{8,11},{9,10},{10,... | collective-permute-start | bytes 589832 | tf_op jit(solution)/shard_map/ppermute | solution.py:284
  276.4 15.0 %collective-permute-start.37 = (bf16[64,256]{1,0:T(8,128)(2,1)S(1)}, bf16[64,256]{1,0:T(8,128)(2,1)S(1)}, u32[]{:S(2)}, u32[]{:S(2)}) collective-permute-start(bf16[64,256]{1,0:T(8,128)(2,1)S(1)} %get-tuple-element.89), channel_id=1, source_target_pairs={{0,12},{4,8},{8,4},{12,0},{16,28},{20,24},{24,20},{28,16},{1,13},{... | collective-permute-start | bytes 98312 | tf_op jit(solution)/shard_map/ppermute | solution.py:294
  278.1 13.2 %collective-permute-start.38 = (bf16[64,256]{1,0:T(8,128)(2,1)S(1)}, bf16[64,256]{1,0:T(8,128)(2,1)S(1)}, u32[]{:S(2)}, u32[]{:S(2)}) collective-permute-start(bf16[64,256]{1,0:T(8,128)(2,1)S(1)} %get-tuple-element.90), channel_id=1, source_target_pairs={{0,16},{4,20},{8,24},{12,28},{16,0},{20,4},{24,8},{28,12},{1,17},{... | collective-permute-start | bytes 98312 | tf_op jit(solution)/shard_map/ppermute | solution.py:294
  (56 other events, 457.8 us)
